TPU v7x, 512 devices: a whole 4x8x8 slice. The times are simulated.
512 devices in a mesh: lat: 64 (over x, z, core), fld: 8 (over y).
Axes of the slice: x: 4, y: 8, z: 8, core: 2. Of those that a mesh axis runs over, the one named last changes fastest.
Arguments:
- fields: bfloat16 [16, 2048, 8192], P('fld', 'lat'), may hold values from -6 to 6
- legendre: bfloat16 [256, 2, 1024, 1024], P('lat', None, 'fld'), may hold values from -0.1875 to 0.1875
- damping: float32 [16], replicated, may hold values from 0.5 to 30
- assignment: int32 [256], replicated, may hold values from 0 to 255, each once
- truncation: int32 [256], replicated, may hold values from 512 to 2048, as said below
Outputs:
- field_out: bfloat16 [16, 2048, 8192], P('fld', 'lat')
- spectra: bfloat16 [256, 2, 16, 2, 1024], P('lat', None, None, None, 'fld')
Inputs may be any that keep to these rules, and one draw needn't show every extreme that they name: `assignment`: a permutation of the wavenumber indices. truncation[0] is 2048 and truncation[255] is 512.
All inputs are finite; a program needn't handle non-finite values.
Results may differ from a plain program's by a relative error of at most 0.009.
Values may be sent and summed in bfloat16 or wider, within the bound.
No kernel may reach another device: no remote copies, remote signals or barrier semaphores. Data moves between devices by JAX's collectives and lax.ppermute only.
A program may use at most 64 MiB of HBM per device.

v0:
```python
import math

import jax
import jax.numpy as jnp
from jax import lax
from jax.sharding import PartitionSpec as P


def from_behind(x, axis, by):
    size = lax.axis_size(axis)
    return lax.ppermute(x, axis, [(i, (i + by) % size) for i in range(size)])


def basis_table(wave_numbers, lon_count):
    positions = jnp.arange(lon_count, dtype=jnp.int32)
    phase = wave_numbers[:, None] * positions[None, :] % lon_count
    angles = phase.astype(jnp.float32) * (2.0 * math.pi / lon_count)
    factor = math.sqrt(2.0 / lon_count)
    return jnp.stack([factor * jnp.cos(angles), -factor * jnp.sin(angles)]).astype(jnp.bfloat16)


def on_device(fields, legendre, damping, assignment, truncation):
    field_count = fields.shape[0]
    lat_rows = fields.shape[1]
    lon_count = fields.shape[2]
    wave_slots = legendre.shape[0]
    pair_slots = legendre.shape[2]
    half_lat = legendre.shape[3]
    field_total = damping.shape[0]
    total_waves = assignment.shape[0]
    total_lat = 2 * half_lat
    columns = 2 * field_count
    lat_devices = lax.axis_size("lat")
    fld_devices = lax.axis_size("fld")
    lat_index = lax.axis_index("lat")
    fld_index = lax.axis_index("fld")
    mirror_step = lat_devices // 2
    northern = lat_index < mirror_step
    fourier_basis = basis_table(assignment + 1, lon_count)
    squared = (fields.astype(jnp.float32) ** 2).astype(jnp.bfloat16)
    fourier = jnp.einsum(
        "flx,rjx->jlfr", squared, fourier_basis, preferred_element_type=jnp.float32
    ).astype(jnp.bfloat16)
    fourier = fourier.reshape(total_waves, lat_rows * columns)
    partner = from_behind(fourier, "lat", mirror_step)
    own_wide = fourier.astype(jnp.float32)
    partner_wide = partner.astype(jnp.float32)
    outgoing = jnp.where(
        northern, (own_wide + partner_wide) * 0.5, (partner_wide - own_wide) * 0.5
    ).astype(jnp.bfloat16)
    received = lax.all_to_all(outgoing, "lat", split_axis=0, concat_axis=1, tiled=True)
    received = received.reshape(wave_slots, total_lat, columns)
    halves = received.reshape(wave_slots, 2, half_lat, columns)
    halves = jnp.transpose(halves, (0, 1, 3, 2))
    coefficient = jnp.einsum(
        "sacl,saql->sacq",
        lax.all_gather(halves, "fld", axis=2, tiled=True),
        legendre,
        preferred_element_type=jnp.float32,
    )
    wave_index = lax.dynamic_slice_in_dim(assignment, lat_index * wave_slots, wave_slots)
    matches = wave_index[:, None] == jnp.arange(total_waves, dtype=jnp.int32)[None, :]
    limits = jnp.sum(jnp.where(matches, truncation[None, :], 0), axis=1)
    pair_global = fld_index * pair_slots + jnp.arange(pair_slots, dtype=jnp.int32)
    degree_offset = 2 * pair_global[None, :] + jnp.arange(2, dtype=jnp.int32)[:, None]
    top_degree = total_waves + 2 * pair_slots * fld_devices - 1
    degree = (wave_index[:, None, None] + 1 + degree_offset[None]).astype(jnp.float32)
    degree_ratio = degree * (degree + 1.0) / float(top_degree * (top_degree + 1))
    kept_mask = degree_offset[None] < limits[:, None, None]
    column_damping = jnp.repeat(damping, 2)
    scaled = coefficient / (
        1.0 + column_damping[None, None, :, None] * (degree_ratio * degree_ratio)[:, :, None, :]
    )
    diffused = jnp.where(kept_mask[:, :, None, :], scaled, 0.0).astype(jnp.bfloat16)
    spectra = diffused.reshape(wave_slots, 2, field_total, 2, pair_slots)
    summed = lax.psum_scatter(
        jnp.einsum("sacq,saql->csal", diffused, legendre, preferred_element_type=jnp.float32),
        "fld",
        scatter_dimension=0,
        tiled=True,
    )
    synthesis = summed.astype(jnp.bfloat16)
    rows_out = jnp.concatenate([synthesis[:, :, 0], synthesis[:, :, 1]], axis=-1)
    outgoing_back = jnp.transpose(rows_out, (1, 2, 0)).reshape(wave_slots, total_lat * columns)
    returned = lax.all_to_all(outgoing_back, "lat", split_axis=1, concat_axis=0, tiled=True)
    partner_back = from_behind(returned, "lat", mirror_step)
    own_back = returned.astype(jnp.float32)
    partner_wide_back = partner_back.astype(jnp.float32)
    gridded = jnp.where(
        northern, own_back + partner_wide_back, partner_wide_back - own_back
    ).astype(jnp.bfloat16)
    gridded = gridded.reshape(total_waves, lat_rows, field_count, 2)
    field_out = jnp.einsum(
        "jlfr,rjx->flx", gridded, fourier_basis, preferred_element_type=jnp.float32
    ).astype(jnp.bfloat16)
    return (field_out, spectra)


def solution(mesh):
    placed = (P("fld", "lat", None), P("lat", None, "fld", None), P(), P(), P())
    return jax.shard_map(
        on_device,
        mesh=mesh,
        in_specs=placed,
        out_specs=(P("fld", "lat", None), P("lat", None, None, None, "fld")),
        check_vma=False,
    )
```

profile of v0, /device:TPU:1, one launch (start us, length us, event | category | flops | bytes accessed | tf_op | source)
XLA Modules:
  0.0 202.6 jit_solution(12673179976172503864)
XLA Ops:
  0.6 0.0 copy-start
  0.6 0.8 broadcast_add_fusion
  1.5 0.0 copy-start.7
  1.5 34.8 %multiply_convert_fusion.1 = (bf16[1,256,8192]{2,1,0:T(8,128)(2,1)S(1)}, bf16[1,256,8192]{2,1,0:T(8,128)(2,1)S(1)}) fusion(s32[256]{0:T(256)S(1)} %broadcast_add_fusion), kind=kLoop, calls=%fused_computation.14 | loop fusion | flops 37748736 | bytes 8389632 | tf_op jit(solution)/shard_map/convert
  36.3 0.0 copy-start.1
  36.3 0.0 copy-start.2
  36.3 0.0 copy-done.7
  36.3 0.0 copy-start.4
  36.3 0.0 copy-start.6
  36.3 0.0 copy-start.5
  36.3 2.7 %fusion.16 = bf16[256,32,2,2]{0,1,2,3:T(8,128)(2,1)S(1)} fusion(bf16[1,256,8192]{2,1,0:T(8,128)(2,1)S(1)} %get-tuple-element.7, bf16[1,256,8192]{2,1,0:T(8,128)(2,1)S(1)} %get-tuple-element.6, bf16[2,32,8192]{2,1,0:T(8,128)(2,1)S(1)} %copy-done.7), kind=kOutput, calls=%fused_computation.24 | convolution fusion | flops 555253760 | bytes 9502720 | tf_op jit(solution)/shard_map/flx,rjx->jlfr/dot_general | solution.py:41
  39.0 0.0 copy-done.1
  39.0 0.5 copy-done.2
  39.5 0.1 copy.36
  39.6 5.5 %collective-permute-start = (bf16[256,128]{0,1:T(8,128)(2,1)S(1)}, bf16[256,128]{0,1:T(8,128)(2,1)S(1)}, u32[]{:S(2)}, u32[]{:S(2)}) collective-permute-start(bf16[256,128]{0,1:T(8,128)(2,1)S(1)} %reshape.160), channel_id=1, source_target_pairs={{0,256},{8,264},{16,272},{24,280},{32,288},{40,296},{48,304},{56,3... | collective-permute-start | bytes 196616 | tf_op jit(solution)/shard_map/ppermute | solution.py:11
  45.1 0.0 copy-done.4
  45.1 0.1 broadcast_add_fusion.1
  45.2 0.0 copy-done.6
  45.2 0.1 broadcast_in_dim.25
  45.2 0.1 mul.134
  45.3 1.3 dynamic-slice
  47.3 0.1 fusion.30
  47.3 0.0 copy-done.5
  47.3 0.2 select_reduce_fusion
  47.5 0.0 collective-permute-done
  47.6 0.7 copy.37
  48.3 14.5 %all-to-all-start = ((bf16[64,4,128]{2,1,0:T(4,128)(2,1)}), bf16[64,4,128]{2,1,0:T(4,128)(2,1)S(1)}, u32[]{:S(2)}, u32[]{:S(2)}) async-start(bf16[64,4,128]{2,1,0:T(4,128)(2,1)} %bitcast.4), calls=%async_computation | async-start | bytes 131072 | tf_op jit(solution)/shard_map/all_to_all | solution.py:51
  62.8 0.1 broadcast_compare_fusion
  62.9 9.7 %all-to-all-done = bf16[64,4,128]{2,1,0:T(4,128)(2,1)S(1)} async-done(((bf16[64,4,128]{2,1,0:T(4,128)(2,1)}), bf16[64,4,128]{2,1,0:T(4,128)(2,1)S(1)}, u32[]{:S(2)}, u32[]{:S(2)}) %all-to-all-start) | async-done | bytes 65568 | tf_op jit(solution)/shard_map/all_to_all | solution.py:51
  72.6 5.5 %reshape_reshape.3 = bf16[4,2,1024,4]{3,2,1,0:T(8,128)(2,1)} reshape(bf16[4,64,128]{2,1,0:T(8,128)(2,1)S(1)} %copy.38) | data formatting | bytes 131072 | tf_op jit(solution)/shard_map/reshape;reshape | solution.py:53
  78.1 2.0 copy.39
  80.1 21.0 %all_gather.3 = bf16[4,2,32,1024]{3,0,1,2:T(4,128)(2,1)S(1)} all-gather(bf16[4,2,4,1024]{3,0,1,2:T(4,128)(2,1)S(1)} %copy.39), channel_id=1, replica_groups=mesh['lat'=64,'fld'=8] {'fld'}, dimensions={2}, use_global_device_ids=true | all-gather | bytes 589824 | tf_op jit(solution)/shard_map/all_gather | solution.py:57
  101.1 0.0 copy-done
  101.1 1.0 fusion.12
  102.0 0.0 copy-start.3
  102.0 0.4 convolution_bitcast_fusion.1
  102.4 48.6 %all-reduce.2 = bf16[32,4,2,1024]{3,0,2,1:T(8,128)(2,1)} all-reduce(f32[32,4,2,1024]{3,0,2,1:T(8,128)S(1)} %convolution_bitcast_fusion.1), channel_id=2, replica_groups=mesh['lat'=64,'fld'=8] {'fld'}, use_global_device_ids=true, to_apply=%region_1.2.clone | all-reduce | flops 262144 | bytes 1572864
  151.0 0.9 dynamic-slice_convert_fusion
  152.0 1.8 copy.42
  153.9 4.9 %all_to_all.29 = bf16[4,64,128]{2,1,0:T(8,128)(2,1)S(1)} reshape(bf16[4,2048,4]{2,1,0:T(8,128)(2,1)} %copy.42) | data formatting | bytes 131072 | tf_op jit(solution)/shard_map/all_to_all | solution.py:85
  158.8 0.0 copy-done.3
  158.8 0.1 copy.43
  158.9 31.0 %all_to_all.35 = bf16[4,64,128]{2,0,1:T(4,128)(2,1)S(1)} all-to-all(bf16[4,64,128]{2,0,1:T(4,128)(2,1)S(1)} %copy.43), channel_id=1, replica_groups=mesh['lat'=64,'fld'=8] {'lat'}, dimensions={1} | all-to-all | bytes 131072 | tf_op jit(solution)/shard_map/all_to_all | solution.py:85
  189.9 0.1 copy.44
  190.0 3.1 %collective-permute-start.1 = (bf16[256,128]{0,1:T(8,128)(2,1)S(1)}, bf16[256,128]{0,1:T(8,128)(2,1)S(1)}, u32[]{:S(2)}, u32[]{:S(2)}) collective-permute-start(bf16[256,128]{0,1:T(8,128)(2,1)S(1)} %copy.44), channel_id=1, source_target_pairs={{0,256},{8,264},{16,272},{24,280},{32,288},{40,296},{48,304},{56,3... | collective-permute-start | bytes 196616 | tf_op jit(solution)/shard_map/ppermute | solution.py:11
  193.1 3.4 %collective-permute-done.1 = bf16[256,128]{0,1:T(8,128)(2,1)S(1)} collective-permute-done((bf16[256,128]{0,1:T(8,128)(2,1)S(1)}, bf16[256,128]{0,1:T(8,128)(2,1)S(1)}, u32[]{:S(2)}, u32[]{:S(2)}) %collective-permute-start.1) | collective-permute-done | bytes 65568 | tf_op jit(solution)/shard_map/ppermute | solution.py:11
  196.6 6.0 %fusion.1 = bf16[2,32,8192]{2,1,0:T(8,128)(2,1)} fusion(bf16[1,256,8192]{2,1,0:T(8,128)(2,1)} %copy-done.2, bf16[1,256,8192]{2,1,0:T(8,128)(2,1)} %copy-done.1, bf16[256,32,2,2]{0,3,2,1:T(2,128)(2,1)S(1)} %reshape.161), kind=kOutput, calls=%fused_computation.5 | convolution fusion | flops 554172416 | bytes 9502720 | tf_op jit(solution)/shard_map/jlfr,rjx->flx/dot_general | solution.py:93
  (9 shorter events, 0.2 us)
Async XLA Ops:
  0.6 100.4 %copy-start = (bf16[4,2,128,1024]{3,2,1,0:T(8,128)(2,1)S(1)}, bf16[4,2,128,1024]{3,2,1,0:T(8,128)(2,1)}, u32[]{:S(2)}) copy-start(bf16[4,2,128,1024]{3,2,1,0:T(8,128)(2,1)} %param.6) | copy-start | bytes 6291460
  1.5 34.8 %copy-start.7 = (bf16[2,32,8192]{2,1,0:T(8,128)(2,1)S(1)}, bf16[2,32,8192]{2,1,0:T(8,128)(2,1)}, u32[]{:S(2)}) copy-start(bf16[2,32,8192]{2,1,0:T(8,128)(2,1)} %param.5) | copy-start | bytes 3145732
  36.3 2.7 %copy-start.1 = (bf16[1,256,8192]{2,1,0:T(8,128)(2,1)}, bf16[1,256,8192]{2,1,0:T(8,128)(2,1)S(1)}, u32[]{:S(2)}) copy-start(bf16[1,256,8192]{2,1,0:T(8,128)(2,1)S(1)} %get-tuple-element.6) | copy-start | bytes 12582916
  36.3 3.2 %copy-start.2 = (bf16[1,256,8192]{2,1,0:T(8,128)(2,1)}, bf16[1,256,8192]{2,1,0:T(8,128)(2,1)S(1)}, u32[]{:S(2)}) copy-start(bf16[1,256,8192]{2,1,0:T(8,128)(2,1)S(1)} %get-tuple-element.7) | copy-start | bytes 12582916
  36.3 8.8 %copy-start.4 = (s32[256]{0:T(256)S(1)}, s32[256]{0:T(256)}, u32[]{:S(2)}) copy-start(s32[256]{0:T(256)} %param.8) | copy-start | bytes 3076
  36.3 8.9 %copy-start.6 = (f32[16]{0:T(128)S(1)}, f32[16]{0:T(128)}, u32[]{:S(2)}) copy-start(f32[16]{0:T(128)} %param.7) | copy-start | bytes 196
  36.3 11.0 %copy-start.5 = (s32[256]{0:T(256)S(1)}, s32[256]{0:T(256)}, u32[]{:S(2)}) copy-start(s32[256]{0:T(256)} %param.9) | copy-start | bytes 3076
  39.6 8.0 %collective-permute-start = (bf16[256,128]{0,1:T(8,128)(2,1)S(1)}, bf16[256,128]{0,1:T(8,128)(2,1)S(1)}, u32[]{:S(2)}, u32[]{:S(2)}) collective-permute-start(bf16[256,128]{0,1:T(8,128)(2,1)S(1)} %reshape.160), channel_id=1, source_target_pairs={{0,256},{8,264},{16,272},{24,280},{32,288},{40,296},{48,304},{56,3... | collective-permute-start | bytes 196616 | tf_op jit(solution)/shard_map/ppermute | solution.py:11
  48.3 24.3 %all-to-all-start = ((bf16[64,4,128]{2,1,0:T(4,128)(2,1)}), bf16[64,4,128]{2,1,0:T(4,128)(2,1)S(1)}, u32[]{:S(2)}, u32[]{:S(2)}) async-start(bf16[64,4,128]{2,1,0:T(4,128)(2,1)} %bitcast.4), calls=%async_computation | async-start | bytes 131072 | tf_op jit(solution)/shard_map/all_to_all | solution.py:51
  102.0 56.8 %copy-start.3 = (bf16[4,2,32,128]{3,2,1,0:T(8,128)(2,1)}, bf16[4,2,32,128]{3,2,1,0:T(8,128)(2,1)S(1)}, u32[]{:S(2)}) copy-start(bf16[4,2,32,128]{3,2,1,0:T(8,128)(2,1)S(1)} %fusion.12) | copy-start | bytes 196612
  190.0 6.5 %collective-permute-start.1 = (bf16[256,128]{0,1:T(8,128)(2,1)S(1)}, bf16[256,128]{0,1:T(8,128)(2,1)S(1)}, u32[]{:S(2)}, u32[]{:S(2)}) collective-permute-start(bf16[256,128]{0,1:T(8,128)(2,1)S(1)} %copy.44), channel_id=1, source_target_pairs={{0,256},{8,264},{16,272},{24,280},{32,288},{40,296},{48,304},{56,3... | collective-permute-start | bytes 196616 | tf_op jit(solution)/shard_map/ppermute | solution.py:11
where the time goes:
time: 203 us
  blocking collectives  101 us (50%)
  other arithmetic  36.1 us (18%)
  starting transfers between devices  23.1 us (11%)
  local copies, waits for them, and re-layouts  18.2 us (9%)
  waiting for transfers between devices  13.1 us (6%)
  matrix products  10 us (5%)
    unnamed x1, blocking collectives  48.6 us
    another operation x1, other arithmetic  34.8 us
    all_to_all x1, blocking collectives, on_device(): lax.all_to_all(outgoing_back, 'lat', split_axis=1, concat_axis=0, tiled=T...  31 us
    all_gather x1, blocking collectives, on_device(): lax.all_gather(halves, 'fld', axis=2, tiled=True)  21 us
    all_to_all x1, starting transfers between devices, on_device(): lax.all_to_all(outgoing, 'lat', split_axis=0, concat_axis=1, tiled=True)  14.5 us
    all_to_all x1, waiting for transfers between devices, on_device(): lax.all_to_all(outgoing, 'lat', split_axis=0, concat_axis=1, tiled=True)  9.7 us
    ppermute x2, starting transfers between devices, from_behind(): return lax.ppermute(x, axis, [(i, (i + by) % size) for i in range(size)])  8.57 us
    dot_general x1, matrix products, on_device(): jnp.einsum('jlfr,rjx->flx', gridded, fourier_basis, preferred_element_typ...  6.01 us
  transfers between devices with their start and end apart: 3, of which 2 were waited for; matrix products, arithmetic and copies ran while one was open for 1% of the time, Pallas kernels for 0%

commit v1 on v0

v1 whole, which is shorter than its diff:
```python
import math

import jax
import jax.numpy as jnp
import numpy as np
from jax import lax
from jax.experimental import pallas as pl
from jax.experimental.pallas import tpu as pltpu
from jax.sharding import PartitionSpec as P

F32 = jnp.float32
BF16 = jnp.bfloat16
RADIX = 8
HALF_ROOT = math.sqrt(0.5)
NT = (((1,), (1,)), ((), ()))
NN = (((1,), (0,)), ((), ()))
CLASS_ORDER = (1, 7, 2, 6, 3, 5, 8, 4)


def dot(a, b, dims):
    return lax.dot_general(a, b, dims, preferred_element_type=F32)


def wave_tables(total_waves, lon_count):
    span = lon_count // RADIX
    per = total_waves // RADIX
    waves = np.concatenate([RADIX * np.arange(per) + c for c in CLASS_ORDER])
    phase = (waves[:, None] * np.arange(span)[None, :]) % lon_count
    angle = phase * (2.0 * np.pi / lon_count)
    sign = np.repeat([1.0, -1.0, 1.0, -1.0, 1.0, -1.0, 1.0, 1.0], per)[:, None]
    factor = math.sqrt(2.0 / lon_count)
    return (
        jnp.asarray((factor * np.cos(angle)).astype(np.float32), BF16),
        jnp.asarray((factor * sign * np.sin(angle)).astype(np.float32), BF16),
    )


def wave_select(assign_row, total_waves):
    per = total_waves // RADIX
    row = lax.broadcasted_iota(jnp.int32, (total_waves, total_waves), 0)
    block = row // per
    cls = jnp.full_like(row, CLASS_ORDER[0])
    for b in range(1, RADIX):
        cls = jnp.where(block == b, CLASS_ORDER[b], cls)
    wave = RADIX * (row % per) + cls - 1
    return jnp.where(wave == assign_row, 1.0, 0.0).astype(BF16)


def forward_kernel(fields_ref, assign_ref, cos_ref, sin_ref, out_ref, z_ref):
    rows, lon_count = fields_ref.shape
    waves, span = cos_ref.shape
    per = waves // RADIX
    tile = 16
    width = 256

    def fold_rows(step, carry):
        r0 = pl.multiple_of(step * tile, tile)
        for x0 in range(0, span, width):
            s = []
            for b in range(RADIX):
                v = fields_ref[pl.ds(r0, tile), b * span + x0 : b * span + x0 + width].astype(F32)
                s.append(v * v)
            e = [s[b] + s[b + 4] for b in range(4)]
            o = [s[b] - s[b + 4] for b in range(4)]
            u = HALF_ROOT * (o[1] - o[3])
            v = HALF_ROOT * (o[1] + o[3])
            even = e[0] + e[2]
            odd = e[1] + e[3]
            parts = (
                o[0] + u, -(o[2] + v),
                e[0] - e[2], e[3] - e[1],
                o[0] - u, o[2] - v,
                even + odd, even - odd,
            )
            for n, part in enumerate(parts):
                z_ref[n, pl.ds(r0, tile), x0 : x0 + width] = part.astype(BF16)
        return carry

    lax.fori_loop(0, rows // tile, fold_rows, 0)
    select = wave_select(assign_ref[...], waves)
    acc = jnp.zeros((2 * rows, waves), F32)
    for p in range(3):
        i0 = 2 * p * per
        zz = z_ref[2 * p : 2 * p + 2].reshape(2 * rows, span)
        dc = dot(zz, cos_ref[i0 : i0 + 2 * per, :], NT)
        ds = dot(zz, sin_ref[i0 : i0 + 2 * per, :], NT)
        real = dc[:rows] + ds[rows:]
        imag = dc[rows:] - ds[:rows]
        lane = lax.broadcasted_iota(jnp.int32, imag.shape, 1)
        imag = jnp.where(lane < per, imag, -imag)
        both = jnp.concatenate([real, imag], axis=0).astype(BF16)
        acc = acc + dot(both, select[i0 : i0 + 2 * per, :], NN)
    for p in range(2):
        i0 = (6 + p) * per
        z = z_ref[6 + p]
        real = dot(z, cos_ref[i0 : i0 + per, :], NT)
        imag = -dot(z, sin_ref[i0 : i0 + per, :], NT)
        both = jnp.concatenate([real, imag], axis=0).astype(BF16)
        acc = acc + dot(both, select[i0 : i0 + per, :], NN)
    out_ref[...] = acc.T.astype(BF16)


def fold_kernel(in_ref, out_ref, x_ref):
    copies = out_ref.shape[0]
    total = in_ref.shape[0]
    slots = 4
    half = total // 2
    x_ref[...] = in_ref[...].astype(F32)
    block = lax.broadcasted_iota(jnp.int32, (8, 128), 1) // 32
    for s in range(slots):
        folded = ([], [])
        for part in range(4):
            north = x_ref[pl.ds(4 * part + s, 8, stride=16), :]
            south = x_ref[pl.ds(half + 4 * part + s, 8, stride=16), :]
            folded[0].append((north + south) * 0.5)
            folded[1].append((north - south) * 0.5)
        for f in range(2):
            for r in range(2):
                source = 2 * r + f
                pair = []
                for a in range(2):
                    rows = None
                    for part in range(4):
                        shift = (32 * (part - source)) % 128
                        moved = folded[a][part]
                        if shift:
                            moved = pltpu.roll(moved, shift, 1)
                        rows = moved if rows is None else jnp.where(block == part, moved, rows)
                    pair.append(rows)
                tile = jnp.concatenate(pair, axis=0).astype(BF16)
                row = ((2 * f + r) * 8 + 2 * s) * 8
                for copy in range(copies):
                    out_ref[copy, row : row + 16, :] = tile


def legendre_kernel(x_ref, table_ref, damping_ref, assign_ref, limit_ref, spectra_ref, out_ref, wide_ref, sums_ref, *, top):
    pairs, degrees, half_lat = table_ref.shape
    columns = spectra_ref.shape[1]
    slots = pairs // 2
    groups = half_lat // 128
    stride = pairs * groups
    slot0 = lax.axis_index("lat") * slots
    first = lax.axis_index("fld") * degrees
    wide_ref[...] = x_ref[...].astype(F32)
    field = lax.broadcasted_iota(jnp.int32, (columns, degrees), 0) // 2
    damp = jnp.zeros((columns, degrees), F32)
    for n in range(columns // 2):
        damp = jnp.where(field == n, damping_ref[n], damp)
    pair_index = first + lax.broadcasted_iota(jnp.int32, (columns, degrees), 1)
    for s in range(slots):
        wave = assign_ref[slot0 + s]
        limit = limit_ref[wave]
        for a in range(2):
            sa = 2 * s + a
            rows = jnp.concatenate(
                [wide_ref[pl.ds(sa * groups + g, columns, stride=stride), :] for g in range(groups)], axis=1
            ).astype(BF16)
            table = table_ref[sa]
            coefficient = dot(rows, table, NT)
            offset = 2 * pair_index + a
            degree = (wave + 1 + offset).astype(F32)
            ratio = degree * (degree + 1.0) / float(top * (top + 1))
            scaled = coefficient / (1.0 + damp * (ratio * ratio))
            diffused = jnp.where(offset < limit, scaled, 0.0).astype(BF16)
            spectra_ref[sa] = diffused
            back = dot(diffused, table, NN)
            for g in range(groups):
                sums_ref[pl.ds(sa * groups + g, columns, stride=stride), :] = back[:, g * 128 : g * 128 + 128]
    out_ref[...] = sums_ref[...].astype(BF16)


def unfold_kernel(in_ref, out_ref, y_ref):
    sources, total, _ = in_ref.shape
    half = total // 2
    block = lax.broadcasted_iota(jnp.int32, (8, 128), 1) // 32

    def summed(row):
        acc = in_ref[0, row : row + 16, :].astype(F32)
        for n in range(1, sources):
            acc = acc + in_ref[n, row : row + 16, :].astype(F32)
        return acc.astype(BF16).astype(F32)

    for s in range(4):
        north, south = {}, {}
        for f in range(2):
            for r in range(2):
                both = summed(((2 * f + r) * 8 + 2 * s) * 8)
                north[2 * r + f] = both[:8] + both[8:]
                south[2 * r + f] = both[:8] - both[8:]
        for part in range(4):
            for base, rows_of in ((0, north), (half, south)):
                rows = None
                for target in range(4):
                    shift = (32 * (target - part)) % 128
                    moved = rows_of[target]
                    if shift:
                        moved = pltpu.roll(moved, shift, 1)
                    rows = moved if rows is None else jnp.where(block == target, moved, rows)
                y_ref[pl.ds(base + 4 * part + s, 8, stride=16), :] = rows
    out_ref[...] = y_ref[...].astype(BF16)


def inverse_kernel(in_ref, assign_ref, cos_ref, sin_ref, out_ref, w_ref):
    rows, lon_count = out_ref.shape
    waves, span = cos_ref.shape
    per = waves // RADIX
    select = wave_select(assign_ref[...], waves)
    slots = in_ref[...].astype(F32).T.astype(BF16)

    def ordered(i0, count):
        return dot(slots, select[i0 : i0 + count, :], NT)

    for p in range(3):
        i0 = 2 * p * per
        g = ordered(i0, 2 * per)
        lane = lax.broadcasted_iota(jnp.int32, g.shape, 1)
        line = lax.broadcasted_iota(jnp.int32, g.shape, 0)
        g = jnp.where((lane >= per) & (line >= rows), -g, g).astype(BF16)
        cc = dot(g, cos_ref[i0 : i0 + 2 * per, :], NN)
        ss = dot(g, sin_ref[i0 : i0 + 2 * per, :], NN)
        w_ref[2 * p] = cc[:rows] - ss[rows:]
        w_ref[2 * p + 1] = ss[:rows] + cc[rows:]
    for p in range(2):
        i0 = (6 + p) * per
        g = ordered(i0, per).astype(BF16)
        w_ref[6 + p] = dot(g[:rows], cos_ref[i0 : i0 + per, :], NN) - dot(g[rows:], sin_ref[i0 : i0 + per, :], NN)

    tile = 16
    width = 256

    def spread_rows(step, carry):
        r0 = pl.multiple_of(step * tile, tile)
        for x0 in range(0, span, width):
            p1, q1, p2, q2, p3, q3, p0, p4 = (w_ref[n, pl.ds(r0, tile), x0 : x0 + width] for n in range(8))
            e0 = p0 + p4
            e1 = p0 - p4
            plus = e0 + p2
            minus = e0 - p2
            low = e1 - q2
            high = e1 + q2
            t0 = p1 + p3
            t2 = q3 - q1
            t1 = HALF_ROOT * ((p1 - q1) - (p3 + q3))
            t3 = HALF_ROOT * ((p3 - q3) - (p1 + q1))
            pieces = (plus + t0, low + t1, minus + t2, high + t3, plus - t0, low - t1, minus - t2, high - t3)
            for b, piece in enumerate(pieces):
                out_ref[pl.ds(r0, tile), b * span + x0 : b * span + x0 + width] = piece.astype(BF16)
        return carry

    lax.fori_loop(0, rows // tile, spread_rows, 0)


def vmem():
    return pl.BlockSpec(memory_space=pltpu.VMEM)


def smem():
    return pl.BlockSpec(memory_space=pltpu.SMEM)


def call(body, name, outs, specs, scratch):
    return pl.pallas_call(
        body,
        name=name,
        out_shape=outs,
        in_specs=specs,
        out_specs=jax.tree.map(lambda _: vmem(), outs),
        scratch_shapes=scratch,
    )


def on_device(fields, legendre, damping, assignment, truncation):
    field_count, lat_rows, lon_count = fields.shape
    wave_slots, _, pair_slots, half_lat = legendre.shape
    total_waves = assignment.shape[0]
    lat_devices = lax.axis_size("lat")
    fld_devices = lax.axis_size("fld")
    field_total = damping.shape[0]
    rows = field_count * lat_rows
    columns = 2 * field_total
    pairs = 2 * wave_slots
    top = total_waves + 2 * pair_slots * fld_devices - 1
    span = lon_count // RADIX
    block = total_waves * 2 * rows // 128
    cos_table, sin_table = wave_tables(total_waves, lon_count)
    assign_row = assignment.reshape(1, total_waves)

    sent = call(
        forward_kernel, "forward", jax.ShapeDtypeStruct((total_waves, 2 * rows), BF16), [vmem()] * 4,
        [pltpu.VMEM((RADIX, rows, span), BF16)],
    )(fields.reshape(rows, lon_count), assign_row, cos_table, sin_table)
    received = lax.all_to_all(sent.reshape(lat_devices, wave_slots, 2 * rows), "lat", 0, 0, tiled=True)
    copies = call(
        fold_kernel, "fold", jax.ShapeDtypeStruct((fld_devices, block, 128), BF16), [vmem()],
        [pltpu.VMEM((total_waves, 2 * rows), F32)],
    )(received.reshape(total_waves, 2 * rows))
    gathered = lax.all_to_all(copies, "fld", 0, 0, tiled=True)
    spectra, partial = call(
        lambda *refs: legendre_kernel(*refs, top=top), "legendre",
        (
            jax.ShapeDtypeStruct((pairs, columns, pair_slots), BF16),
            jax.ShapeDtypeStruct((fld_devices * block, 128), BF16),
        ),
        [vmem(), vmem(), smem(), smem(), smem()],
        [pltpu.VMEM((fld_devices * block, 128), F32), pltpu.VMEM((fld_devices * block, 128), F32)],
    )(
        gathered.reshape(fld_devices * block, 128),
        legendre.reshape(pairs, pair_slots, half_lat),
        damping,
        assignment,
        truncation,
    )
    parts = lax.all_to_all(partial.reshape(fld_devices, block, 128), "fld", 0, 0, tiled=True)
    outgoing = call(
        unfold_kernel, "unfold", jax.ShapeDtypeStruct((total_waves, 2 * rows), BF16), [vmem()],
        [pltpu.VMEM((total_waves, 2 * rows), F32)],
    )(parts)
    returned = lax.all_to_all(outgoing.reshape(lat_devices, wave_slots, 2 * rows), "lat", 0, 0, tiled=True)
    field_out = call(
        inverse_kernel, "inverse", jax.ShapeDtypeStruct((rows, lon_count), BF16), [vmem()] * 4,
        [pltpu.VMEM((RADIX, rows, span), F32)],
    )(returned.reshape(total_waves, 2 * rows), assign_row, cos_table, sin_table)
    return (
        field_out.reshape(field_count, lat_rows, lon_count),
        spectra.reshape(wave_slots, 2, field_total, 2, pair_slots),
    )


def solution(mesh):
    placed = (P("fld", "lat", None), P("lat", None, "fld", None), P(), P(), P())
    return jax.shard_map(
        on_device,
        mesh=mesh,
        in_specs=placed,
        out_specs=(P("fld", "lat", None), P("lat", None, None, None, "fld")),
        check_vma=False,
    )
```

time: 203 us -> 104 us (0.51)
  other arithmetic: 36.1 us -> 0 us
  starting transfers between devices: 23.1 us -> 0 us
  local copies, waits for them, and re-layouts: 18.2 us -> 0 us
  Pallas kernels: 0 us -> 17 us
  blocking collectives: 101 us -> 85.5 us
  waiting for transfers between devices: 13.1 us -> 0 us
  matrix products: 10 us -> 0 us
    all_to_all x1 -> x4, blocking collectives: 31 us -> 85.5 us  [the longest x1 24.7 us: on_device(): lax.all_to_all(sent.reshape(lat_devices, wave_slots, 2 * rows), 'lat', 0,...]
    unnamed x1 -> x0, blocking collectives: 48.6 us -> none
    another operation x1 -> x0, other arithmetic: 34.8 us -> none
    all_gather x1 -> x0, blocking collectives: 21 us -> none  [on_device(): lax.all_gather(halves, 'fld', axis=2, tiled=True)]
    pallas_call x0 -> x5, Pallas kernels: none -> 17 us  [the longest x1 5.61 us: on_device(): call(lambda *refs: legendre_kernel(*refs, top=top), 'legendre', (jax.Shap...]
    all_to_all x1 -> x0, starting transfers between devices: 14.5 us -> none  [on_device(): lax.all_to_all(outgoing, 'lat', split_axis=0, concat_axis=1, tiled=True)]
    dot_general x4 -> x0, matrix products: 10 us -> none  [the longest x1 6.01 us: on_device(): jnp.einsum('jlfr,rjx->flx', gridded, fourier_basis, preferred_element_typ...]
    all_to_all x1 -> x0, waiting for transfers between devices: 9.7 us -> none  [on_device(): lax.all_to_all(outgoing, 'lat', split_axis=0, concat_axis=1, tiled=True)]
  transfers between devices with their start and end apart: 3 -> 0, of which waited for: 2 -> 0; matrix products, arithmetic and copies ran while one was open for 1% -> 0% of each run, Pallas kernels for 0% -> 0%
where the time goes in v1:
time: 104 us; the launch traced here: 103 us
  blocking collectives  85.5 us (82%)
  Pallas kernels  17 us (16%)
    all_to_all x1, blocking collectives, on_device(): lax.all_to_all(sent.reshape(lat_devices, wave_slots, 2 * rows), 'lat', 0,...  24.7 us
    all_to_all x1, blocking collectives, on_device(): gathered = lax.all_to_all(copies, 'fld', 0, 0, tiled=True)  23.6 us
    all_to_all x1, blocking collectives, on_device(): lax.all_to_all(partial.reshape(fld_devices, block, 128), 'fld', 0, 0, til...  19 us
    all_to_all x1, blocking collectives, on_device(): lax.all_to_all(outgoing.reshape(lat_devices, wave_slots, 2 * rows), 'lat'...  18.2 us
    pallas_call x1, Pallas kernels, on_device(): call(lambda *refs: legendre_kernel(*refs, top=top), 'legendre', (jax.Shap...  5.61 us
    pallas_call x1, Pallas kernels, on_device(): call(forward_kernel, 'forward', jax.ShapeDtypeStruct((total_waves, 2 * ro...  3.92 us
    pallas_call x1, Pallas kernels, on_device(): call(inverse_kernel, 'inverse', jax.ShapeDtypeStruct((rows, lon_count), B...  3.8 us

profile of v1, /device:TPU:1, one launch (start us, length us, event | category | flops | bytes accessed | tf_op | source)
XLA Modules:
  0.0 103.1 jit_solution(3429075699014902921)
XLA Ops:
  0.6 3.9 %forward.1 = bf16[256,128]{1,0:T(8,128)(2,1)} custom-call(bf16[64,8192]{1,0:T(8,128)(2,1)} %bitcast.13, s32[1,256]{1,0:T(1,128)} %bitcast.20, bf16[256,1024]{1,0:T(8,128)(2,1)} %constant.4.clone.cos_ref, bf16[256,1024]{1,0:T(8,128)(2,1)} %constant.5.clone.sin_ref), custom_call_target="tpu_custom_call" | custom-call | tf_op jit(solution)/shard_map/forward/pallas_call | solution.py:288
  4.6 24.7 %all_to_all.20 = bf16[64,4,128]{2,1,0:T(4,128)(2,1)} all-to-all(bf16[64,4,128]{2,1,0:T(4,128)(2,1)} %bitcast.19), channel_id=1, replica_groups=mesh['lat'=64,'fld'=8] {'lat'}, dimensions={0} | all-to-all | bytes 131072 | tf_op jit(solution)/shard_map/all_to_all | solution.py:292
  29.2 1.8 %fold.1 = bf16[8,256,128]{2,1,0:T(8,128)(2,1)} custom-call(bf16[256,128]{1,0:T(8,128)(2,1)} %bitcast.17), custom_call_target="tpu_custom_call" | custom-call | tf_op jit(solution)/shard_map/fold/pallas_call | solution.py:293
  31.0 23.6 %all_to_all.21 = bf16[8,256,128]{2,1,0:T(8,128)(2,1)} all-to-all(bf16[8,256,128]{2,1,0:T(8,128)(2,1)} %fold.1), channel_id=1, replica_groups=mesh['lat'=64,'fld'=8] {'fld'}, dimensions={0} | all-to-all | bytes 1048576 | tf_op jit(solution)/shard_map/all_to_all | solution.py:297
  54.6 5.6 %legendre.1 = (bf16[8,32,128]{2,1,0:T(8,128)(2,1)}, bf16[2048,128]{1,0:T(8,128)(2,1)}) custom-call(bf16[2048,128]{1,0:T(8,128)(2,1)} %bitcast.11, bf16[8,128,1024]{2,1,0:T(8,128)(2,1)} %bitcast.12, f32[16]{0:T(128)} %refs_2_.1, s32[256]{0:T(256)} %refs_3_.1, s32[256]{0:T(256)} %refs_4_.1), custom_call_target="tpu_custom_call" | custom-call | tf_op jit(solution)/shard_map/legendre/pallas_call | solution.py:298
  60.2 19.0 %all_to_all.22.in_ref = bf16[8,256,128]{2,1,0:T(8,128)(2,1)} all-to-all(bf16[8,256,128]{2,1,0:T(8,128)(2,1)} %bitcast.15), channel_id=1, replica_groups=mesh['lat'=64,'fld'=8] {'fld'}, dimensions={0} | all-to-all | bytes 1048576 | tf_op jit(solution)/shard_map/all_to_all | solution.py:313
  79.3 1.9 %unfold.1 = bf16[256,128]{1,0:T(8,128)(2,1)} custom-call(bf16[8,256,128]{2,1,0:T(8,128)(2,1)} %all_to_all.22.in_ref), custom_call_target="tpu_custom_call" | custom-call | tf_op jit(solution)/shard_map/unfold/pallas_call | solution.py:314
  81.2 18.2 %all_to_all.23 = bf16[64,4,128]{2,1,0:T(4,128)(2,1)} all-to-all(bf16[64,4,128]{2,1,0:T(4,128)(2,1)} %bitcast.18), channel_id=1, replica_groups=mesh['lat'=64,'fld'=8] {'lat'}, dimensions={0} | all-to-all | bytes 131072 | tf_op jit(solution)/shard_map/all_to_all | solution.py:318
  99.3 3.8 %inverse.1 = bf16[64,8192]{1,0:T(8,128)(2,1)} custom-call(bf16[256,128]{1,0:T(8,128)(2,1)} %bitcast.16, s32[1,256]{1,0:T(1,128)} %bitcast.21, bf16[256,1024]{1,0:T(8,128)(2,1)} %constant.4.clone.cos_ref, bf16[256,1024]{1,0:T(8,128)(2,1)} %constant.5.clone.sin_ref), custom_call_target="tpu_custom_call" | custom-call | tf_op jit(solution)/shard_map/inverse/pallas_call | solution.py:319

commit v2 on v1

--- a/solution.py
+++ b/solution.py
@@ -46,15 +46,31 @@
     return jnp.where(wave == assign_row, 1.0, 0.0).astype(BF16)
 
 
-def forward_kernel(fields_ref, assign_ref, cos_ref, sin_ref, out_ref, z_ref):
+def forward_kernel(
+    fields_hbm, assign_hbm, cos_hbm, sin_hbm, table_hbm,
+    out_ref, assign_ref, cos_ref, sin_ref, table_ref, fields_ref, z_ref, sems,
+):
     rows, lon_count = fields_ref.shape
     waves, span = cos_ref.shape
     per = waves // RADIX
     tile = 16
     width = 256
+    steps = rows // tile
+
+    def rows_copy(step):
+        at = pl.ds(pl.multiple_of(step * tile, tile), tile)
+        return pltpu.make_async_copy(fields_hbm.at[at], fields_ref.at[at], sems.at[step])
+
+    for step in range(steps):
+        rows_copy(step).start()
+    moves = ((assign_hbm, assign_ref), (cos_hbm, cos_ref), (sin_hbm, sin_ref), (table_hbm, table_ref))
+    loads = [pltpu.make_async_copy(*move, sems.at[steps + n]) for n, move in enumerate(moves)]
+    for load in loads:
+        load.start()
 
     def fold_rows(step, carry):
         r0 = pl.multiple_of(step * tile, tile)
+        rows_copy(step).wait()
         for x0 in range(0, span, width):
             s = []
             for b in range(RADIX):
@@ -76,7 +92,9 @@
                 z_ref[n, pl.ds(r0, tile), x0 : x0 + width] = part.astype(BF16)
         return carry
 
-    lax.fori_loop(0, rows // tile, fold_rows, 0)
+    lax.fori_loop(0, steps, fold_rows, 0)
+    for load in loads[:3]:
+        load.wait()
     select = wave_select(assign_ref[...], waves)
     acc = jnp.zeros((2 * rows, waves), F32)
     for p in range(3):
@@ -98,6 +116,7 @@
         both = jnp.concatenate([real, imag], axis=0).astype(BF16)
         acc = acc + dot(both, select[i0 : i0 + per, :], NN)
     out_ref[...] = acc.T.astype(BF16)
+    loads[3].wait()
 
 
 def fold_kernel(in_ref, out_ref, x_ref):
@@ -200,7 +219,7 @@
     out_ref[...] = y_ref[...].astype(BF16)
 
 
-def inverse_kernel(in_ref, assign_ref, cos_ref, sin_ref, out_ref, w_ref):
+def inverse_kernel(in_ref, assign_ref, cos_ref, sin_ref, out_hbm, w_ref, out_ref, sems):
     rows, lon_count = out_ref.shape
     waves, span = cos_ref.shape
     per = waves // RADIX
@@ -227,6 +246,10 @@
 
     tile = 16
     width = 256
+
+    def rows_copy(step):
+        at = pl.ds(pl.multiple_of(step * tile, tile), tile)
+        return pltpu.make_async_copy(out_ref.at[at], out_hbm.at[at], sems.at[step])
 
     def spread_rows(step, carry):
         r0 = pl.multiple_of(step * tile, tile)
@@ -245,27 +268,38 @@
             pieces = (plus + t0, low + t1, minus + t2, high + t3, plus - t0, low - t1, minus - t2, high - t3)
             for b, piece in enumerate(pieces):
                 out_ref[pl.ds(r0, tile), b * span + x0 : b * span + x0 + width] = piece.astype(BF16)
+        rows_copy(step).start()
         return carry
 
     lax.fori_loop(0, rows // tile, spread_rows, 0)
-
-
-def vmem():
-    return pl.BlockSpec(memory_space=pltpu.VMEM)
-
-
-def smem():
-    return pl.BlockSpec(memory_space=pltpu.SMEM)
-
-
-def call(body, name, outs, specs, scratch):
+    for step in range(rows // tile):
+        rows_copy(step).wait()
+
+
+VMEM = pl.BlockSpec(memory_space=pltpu.VMEM)
+SMEM = pl.BlockSpec(memory_space=pltpu.SMEM)
+HBM = pl.BlockSpec(memory_space=pltpu.HBM)
+
+
+def in_vmem(array):
+    return pltpu.with_memory_space_constraint(array, pltpu.VMEM)
+
+
+def in_hbm(array):
+    return pltpu.with_memory_space_constraint(array, pltpu.HBM)
+
+
+def call(body, name, outs, specs, scratch, out_specs=None):
+    if out_specs is None:
+        out_specs = tuple(VMEM for _ in outs)
     return pl.pallas_call(
         body,
         name=name,
         out_shape=outs,
         in_specs=specs,
-        out_specs=jax.tree.map(lambda _: vmem(), outs),
+        out_specs=out_specs,
         scratch_shapes=scratch,
+        compiler_params=pltpu.CompilerParams(vmem_limit_bytes=16 << 20),
     )
 
 
@@ -281,45 +315,59 @@
     pairs = 2 * wave_slots
     top = total_waves + 2 * pair_slots * fld_devices - 1
     span = lon_count // RADIX
+    steps = rows // 16
     block = total_waves * 2 * rows // 128
-    cos_table, sin_table = wave_tables(total_waves, lon_count)
-    assign_row = assignment.reshape(1, total_waves)
-
-    sent = call(
-        forward_kernel, "forward", jax.ShapeDtypeStruct((total_waves, 2 * rows), BF16), [vmem()] * 4,
-        [pltpu.VMEM((RADIX, rows, span), BF16)],
-    )(fields.reshape(rows, lon_count), assign_row, cos_table, sin_table)
+    by_wave = pltpu.VMEM((total_waves, 2 * rows), BF16)
+    wide = pltpu.VMEM((total_waves, 2 * rows), F32)
+    gathered_wide = pltpu.VMEM((fld_devices * block, 128), F32)
+
+    sent, assign_row, cos_table, sin_table, table = call(
+        forward_kernel, "forward",
+        (
+            by_wave,
+            pltpu.VMEM((1, total_waves), jnp.int32),
+            pltpu.VMEM((total_waves, span), BF16),
+            pltpu.VMEM((total_waves, span), BF16),
+            pltpu.VMEM((pairs, pair_slots, half_lat), BF16),
+        ),
+        [HBM] * 5,
+        [
+            pltpu.VMEM((rows, lon_count), BF16),
+            pltpu.VMEM((RADIX, rows, span), BF16),
+            pltpu.SemaphoreType.DMA((steps + 4,)),
+        ],
+    )(
+        in_hbm(fields.reshape(rows, lon_count)),
+        in_hbm(assignment.reshape(1, total_waves)),
+        *map(in_hbm, wave_tables(total_waves, lon_count)),
+        in_hbm(legendre.reshape(pairs, pair_slots, half_lat)),
+    )
     received = lax.all_to_all(sent.reshape(lat_devices, wave_slots, 2 * rows), "lat", 0, 0, tiled=True)
-    copies = call(
-        fold_kernel, "fold", jax.ShapeDtypeStruct((fld_devices, block, 128), BF16), [vmem()],
-        [pltpu.VMEM((total_waves, 2 * rows), F32)],
-    )(received.reshape(total_waves, 2 * rows))
+    (copies,) = call(
+        fold_kernel, "fold", (pltpu.VMEM((fld_devices, block, 128), BF16),), [VMEM], [wide]
+    )(in_vmem(received.reshape(total_waves, 2 * rows)))
     gathered = lax.all_to_all(copies, "fld", 0, 0, tiled=True)
     spectra, partial = call(
         lambda *refs: legendre_kernel(*refs, top=top), "legendre",
         (
             jax.ShapeDtypeStruct((pairs, columns, pair_slots), BF16),
-            jax.ShapeDtypeStruct((fld_devices * block, 128), BF16),
+            pltpu.VMEM((fld_devices * block, 128), BF16),
         ),
-        [vmem(), vmem(), smem(), smem(), smem()],
-        [pltpu.VMEM((fld_devices * block, 128), F32), pltpu.VMEM((fld_devices * block, 128), F32)],
-    )(
-        gathered.reshape(fld_devices * block, 128),
-        legendre.reshape(pairs, pair_slots, half_lat),
-        damping,
-        assignment,
-        truncation,
-    )
+        [VMEM, VMEM, SMEM, SMEM, SMEM],
+        [gathered_wide, gathered_wide],
+    )(in_vmem(gathered.reshape(fld_devices * block, 128)), in_vmem(table), damping, assignment, truncation)
     parts = lax.all_to_all(partial.reshape(fld_devices, block, 128), "fld", 0, 0, tiled=True)
-    outgoing = call(
-        unfold_kernel, "unfold", jax.ShapeDtypeStruct((total_waves, 2 * rows), BF16), [vmem()],
-        [pltpu.VMEM((total_waves, 2 * rows), F32)],
-    )(parts)
+    (outgoing,) = call(unfold_kernel, "unfold", (by_wave,), [VMEM], [wide])(in_vmem(parts))
     returned = lax.all_to_all(outgoing.reshape(lat_devices, wave_slots, 2 * rows), "lat", 0, 0, tiled=True)
-    field_out = call(
-        inverse_kernel, "inverse", jax.ShapeDtypeStruct((rows, lon_count), BF16), [vmem()] * 4,
-        [pltpu.VMEM((RADIX, rows, span), F32)],
-    )(returned.reshape(total_waves, 2 * rows), assign_row, cos_table, sin_table)
+    (field_out,) = call(
+        inverse_kernel, "inverse", (jax.ShapeDtypeStruct((rows, lon_count), BF16),), [VMEM] * 4,
+        [
+            pltpu.VMEM((RADIX, rows, span), F32),
+            pltpu.VMEM((rows, lon_count), BF16),
+            pltpu.SemaphoreType.DMA((steps,)),
+        ],
+        (HBM,),
+    )(in_vmem(returned.reshape(total_waves, 2 * rows)), in_vmem(assign_row), in_vmem(cos_table), in_vmem(sin_table))
     return (
         field_out.reshape(field_count, lat_rows, lon_count),
         spectra.reshape(wave_slots, 2, field_total, 2, pair_slots),

time: 104 us -> 92.4 us (0.89)
  Pallas kernels: 17 us -> 9.79 us
  blocking collectives: 85.5 us -> 81.6 us
    pallas_call x4, Pallas kernels: 11.4 us -> 5.72 us  [the longest x1 3.01 us: on_device(): call(forward_kernel, 'forward', (by_wave, pltpu.VMEM((1, total_waves), jn...]
    all_to_all x1, blocking collectives: 19 us -> 17.3 us  [on_device(): lax.all_to_all(partial.reshape(fld_devices, block, 128), 'fld', 0, 0, til...]
    pallas_call x1, Pallas kernels: 5.61 us -> 4.07 us  [on_device(): call(lambda *refs: legendre_kernel(*refs, top=top), 'legendre', (jax.Shap...]
    all_to_all x1, blocking collectives: 18.2 us -> 16.7 us  [on_device(): lax.all_to_all(outgoing.reshape(lat_devices, wave_slots, 2 * rows), 'lat'...]
where the time goes in v2:
time: 92.4 us; the launch traced here: 92.1 us
  blocking collectives  81.6 us (88%)
  Pallas kernels  9.79 us (11%)
    all_to_all x1, blocking collectives, on_device(): lax.all_to_all(sent.reshape(lat_devices, wave_slots, 2 * rows), 'lat', 0,...  24.4 us
    all_to_all x1, blocking collectives, on_device(): gathered = lax.all_to_all(copies, 'fld', 0, 0, tiled=True)  23.3 us
    all_to_all x1, blocking collectives, on_device(): lax.all_to_all(partial.reshape(fld_devices, block, 128), 'fld', 0, 0, til...  17.3 us
    all_to_all x1, blocking collectives, on_device(): lax.all_to_all(outgoing.reshape(lat_devices, wave_slots, 2 * rows), 'lat'...  16.7 us
    pallas_call x1, Pallas kernels, on_device(): call(lambda *refs: legendre_kernel(*refs, top=top), 'legendre', (jax.Shap...  4.07 us
    pallas_call x1, Pallas kernels, on_device(): call(forward_kernel, 'forward', (by_wave, pltpu.VMEM((1, total_waves), jn...  3.01 us
    pallas_call x1, Pallas kernels, on_device(): call(inverse_kernel, 'inverse', (jax.ShapeDtypeStruct((rows, lon_count),...  2.36 us

profile of v2, /device:TPU:1, one launch (start us, length us, event | category | flops | bytes accessed | tf_op | source)
XLA Modules:
  0.0 92.1 jit_solution(17006217212355928381)
XLA Ops:
  0.6 0.0 copy-start
  0.6 0.0 copy-start.1
  0.7 0.0 copy-start.2
  0.7 3.0 %forward.1 = (bf16[256,128]{1,0:T(8,128)(2,1)S(1)}, s32[1,256]{1,0:T(1,128)S(1)}, bf16[256,1024]{1,0:T(8,128)(2,1)S(1)}, bf16[256,1024]{1,0:T(8,128)(2,1)S(1)}, bf16[8,128,1024]{2,1,0:T(8,128)(2,1)S(1)}) custom-call(bf16[64,8192]{1,0:T(8,128)(2,1)} %bitcast.19, s32[1,256]{1,0:T(1,128)} %bitcast.17, bf16[256,1024]{1,0:T(8,128)(2,1)} %constant.4.clone.cos_hbm, ...), custom_call_target="tpu_custom_call" | custom-call | tf_op jit(solution)/shard_map/forward/pallas_call | solution.py:324
  3.7 24.4 %all_to_all.20 = bf16[64,4,128]{2,1,0:T(4,128)(2,1)S(1)} all-to-all(bf16[64,4,128]{2,1,0:T(4,128)(2,1)S(1)} %bitcast.16), channel_id=1, replica_groups=mesh['lat'=64,'fld'=8] {'lat'}, dimensions={0} | all-to-all | bytes 131072 | tf_op jit(solution)/shard_map/all_to_all | solution.py:345
  28.0 0.2 fold.1
  28.2 23.3 %all_to_all.21 = bf16[8,256,128]{2,1,0:T(8,128)(2,1)S(1)} all-to-all(bf16[8,256,128]{2,1,0:T(8,128)(2,1)S(1)} %fold.1), channel_id=1, replica_groups=mesh['lat'=64,'fld'=8] {'fld'}, dimensions={0} | all-to-all | bytes 1048576 | tf_op jit(solution)/shard_map/all_to_all | solution.py:349
  51.5 0.0 copy-done
  51.5 0.0 copy-done.1
  51.5 0.0 copy-done.2
  51.5 4.1 %legendre.1 = (bf16[8,32,128]{2,1,0:T(8,128)(2,1)}, bf16[2048,128]{1,0:T(8,128)(2,1)S(1)}) custom-call(bf16[2048,128]{1,0:T(8,128)(2,1)S(1)} %bitcast.11, bf16[8,128,1024]{2,1,0:T(8,128)(2,1)S(1)} %get-tuple-element.10.refs_1_, f32[16]{0:T(128)S(1)} %copy-done.2, s32[256]{0:T(256)S(1)} %copy-done, s32[256]{0:T(256)S(1)} %copy-done.1), custom_call_target="tpu_custom_call" | custom-call | tf_op jit(solution)/shard_map/legendre/pallas_call | solution.py:350
  55.6 17.3 %all_to_all.22.in_ref = bf16[8,256,128]{2,1,0:T(8,128)(2,1)S(1)} all-to-all(bf16[8,256,128]{2,1,0:T(8,128)(2,1)S(1)} %bitcast.12), channel_id=1, replica_groups=mesh['lat'=64,'fld'=8] {'fld'}, dimensions={0} | all-to-all | bytes 1048576 | tf_op jit(solution)/shard_map/all_to_all | solution.py:359
  72.9 0.2 unfold.1
  73.1 16.7 %all_to_all.23 = bf16[64,4,128]{2,1,0:T(4,128)(2,1)S(1)} all-to-all(bf16[64,4,128]{2,1,0:T(4,128)(2,1)S(1)} %bitcast.15), channel_id=1, replica_groups=mesh['lat'=64,'fld'=8] {'lat'}, dimensions={0} | all-to-all | bytes 131072 | tf_op jit(solution)/shard_map/all_to_all | solution.py:361
  89.8 2.4 %inverse.1 = bf16[64,8192]{1,0:T(8,128)(2,1)} custom-call(bf16[256,128]{1,0:T(8,128)(2,1)S(1)} %bitcast.13, s32[1,256]{1,0:T(1,128)S(1)} %get-tuple-element.12.assign_ref, bf16[256,1024]{1,0:T(8,128)(2,1)S(1)} %get-tuple-element.13.cos_ref, bf16[256,1024]{1,0:T(8,128)(2,1)S(1)} %get-tuple-element.14.sin_ref), custom_call_target="tpu_custom_call" | custom-call | tf_op jit(solution)/shard_map/inverse/pallas_call | solution.py:362
Async XLA Ops:
  0.6 50.9 %copy-start = (s32[256]{0:T(256)S(1)}, s32[256]{0:T(256)}, u32[]{:S(2)}) copy-start(s32[256]{0:T(256)} %refs_3_.1) | copy-start | bytes 3076
  0.6 50.8 %copy-start.1 = (s32[256]{0:T(256)S(1)}, s32[256]{0:T(256)}, u32[]{:S(2)}) copy-start(s32[256]{0:T(256)} %refs_4_.1) | copy-start | bytes 3076
  0.7 50.8 %copy-start.2 = (f32[16]{0:T(128)S(1)}, f32[16]{0:T(128)}, u32[]{:S(2)}) copy-start(f32[16]{0:T(128)} %refs_2_.1) | copy-start | bytes 196

commit v3 on v2

--- a/solution.py
+++ b/solution.py
@@ -21,37 +21,27 @@
     return lax.dot_general(a, b, dims, preferred_element_type=F32)
 
 
-def wave_tables(total_waves, lon_count):
+def wave_table(total_waves, lon_count):
     span = lon_count // RADIX
     per = total_waves // RADIX
-    waves = np.concatenate([RADIX * np.arange(per) + c for c in CLASS_ORDER])
-    phase = (waves[:, None] * np.arange(span)[None, :]) % lon_count
-    angle = phase * (2.0 * np.pi / lon_count)
-    sign = np.repeat([1.0, -1.0, 1.0, -1.0, 1.0, -1.0, 1.0, 1.0], per)[:, None]
     factor = math.sqrt(2.0 / lon_count)
-    return (
-        jnp.asarray((factor * np.cos(angle)).astype(np.float32), BF16),
-        jnp.asarray((factor * sign * np.sin(angle)).astype(np.float32), BF16),
-    )
-
-
-def wave_select(assign_row, total_waves):
-    per = total_waves // RADIX
-    row = lax.broadcasted_iota(jnp.int32, (total_waves, total_waves), 0)
-    block = row // per
-    cls = jnp.full_like(row, CLASS_ORDER[0])
-    for b in range(1, RADIX):
-        cls = jnp.where(block == b, CLASS_ORDER[b], cls)
-    wave = RADIX * (row % per) + cls - 1
-    return jnp.where(wave == assign_row, 1.0, 0.0).astype(BF16)
+    blocks = []
+    for classes in ((1, 7), (2, 6), (3, 5), (8,), (4,)):
+        waves = np.concatenate([RADIX * np.arange(per) + c for c in classes])
+        angle = (waves[:, None] * np.arange(span)[None, :] % lon_count) * (2.0 * np.pi / lon_count)
+        sign = np.where(np.arange(len(waves)) < per, 1.0, -1.0)[:, None]
+        blocks += [factor * np.cos(angle), factor * sign * np.sin(angle)]
+    return jnp.asarray(np.concatenate(blocks).astype(np.float32), BF16)
 
 
 def forward_kernel(
-    fields_hbm, assign_hbm, cos_hbm, sin_hbm, table_hbm,
-    out_ref, assign_ref, cos_ref, sin_ref, table_ref, fields_ref, z_ref, sems,
+    fields_hbm, assign_hbm, trig_hbm, table_hbm, damping_hbm, limit_hbm,
+    out_ref, select_ref, trig_ref, table_ref, scale_ref,
+    fields_ref, z_ref, assign_ref, damping_ref, slot_ref, limit_ref, sems, *, top,
 ):
     rows, lon_count = fields_ref.shape
-    waves, span = cos_ref.shape
+    waves = select_ref.shape[0]
+    span = trig_ref.shape[1]
     per = waves // RADIX
     tile = 16
     width = 256
@@ -61,12 +51,47 @@
         at = pl.ds(pl.multiple_of(step * tile, tile), tile)
         return pltpu.make_async_copy(fields_hbm.at[at], fields_ref.at[at], sems.at[step])
 
+    moves = (
+        (damping_hbm, damping_ref), (assign_hbm, slot_ref), (limit_hbm, limit_ref), (assign_hbm, assign_ref),
+        (trig_hbm, trig_ref), (table_hbm, table_ref),
+    )
+    loads = [pltpu.make_async_copy(*move, sems.at[steps + n]) for n, move in enumerate(moves)]
+    for load in loads[:4]:
+        load.start()
     for step in range(steps):
         rows_copy(step).start()
-    moves = ((assign_hbm, assign_ref), (cos_hbm, cos_ref), (sin_hbm, sin_ref), (table_hbm, table_ref))
-    loads = [pltpu.make_async_copy(*move, sems.at[steps + n]) for n, move in enumerate(moves)]
-    for load in loads:
-        load.start()
+    loads[4].start()
+    for load in loads[:4]:
+        load.wait()
+
+    pairs, columns, degrees = scale_ref.shape
+    slots = pairs // 2
+    slot0 = lax.axis_index("lat") * slots
+    first = lax.axis_index("fld") * degrees
+    field = lax.broadcasted_iota(jnp.int32, (columns, degrees), 0) // 2
+    damp = jnp.zeros((columns, degrees), F32)
+    for n in range(columns // 2):
+        damp = jnp.where(field == n, damping_ref[0, n], damp)
+    pair_index = first + lax.broadcasted_iota(jnp.int32, (8, degrees), 1)
+    for s in range(slots):
+        wave = slot_ref[0, slot0 + s]
+        limit = limit_ref[0, wave]
+        for a in range(2):
+            offset = 2 * pair_index + a
+            degree = (wave + 1 + offset).astype(F32)
+            ratio = degree * (degree + 1.0) / float(top * (top + 1))
+            square = ratio * ratio
+            kept = offset < limit
+            for c in range(0, columns, 8):
+                factor = 1.0 / (1.0 + damp[c : c + 8] * square)
+                scale_ref[2 * s + a, c : c + 8, :] = jnp.where(kept, factor, 0.0)
+
+    wave_of = RADIX * lax.broadcasted_iota(jnp.int32, (per, waves), 0) - 1
+    for n, cls in enumerate(CLASS_ORDER):
+        hit = (wave_of + cls) == assign_ref[...]
+        select_ref[n * per : (n + 1) * per, :] = jnp.where(hit, 1.0, 0.0).astype(BF16)
+
+    loads[5].start()
 
     def fold_rows(step, carry):
         r0 = pl.multiple_of(step * tile, tile)
@@ -93,30 +118,26 @@
         return carry
 
     lax.fori_loop(0, steps, fold_rows, 0)
-    for load in loads[:3]:
-        load.wait()
-    select = wave_select(assign_ref[...], waves)
+    loads[4].wait()
     acc = jnp.zeros((2 * rows, waves), F32)
     for p in range(3):
-        i0 = 2 * p * per
+        wide = 2 * per
         zz = z_ref[2 * p : 2 * p + 2].reshape(2 * rows, span)
-        dc = dot(zz, cos_ref[i0 : i0 + 2 * per, :], NT)
-        ds = dot(zz, sin_ref[i0 : i0 + 2 * per, :], NT)
-        real = dc[:rows] + ds[rows:]
-        imag = dc[rows:] - ds[:rows]
+        d = dot(zz, trig_ref[2 * p * wide : 2 * (p + 1) * wide, :], NT)
+        turned = pltpu.roll(d, wide, 1)
+        real = d[:rows] + turned[rows:]
+        imag = d[rows:] - turned[:rows]
         lane = lax.broadcasted_iota(jnp.int32, imag.shape, 1)
-        imag = jnp.where(lane < per, imag, -imag)
-        both = jnp.concatenate([real, imag], axis=0).astype(BF16)
-        acc = acc + dot(both, select[i0 : i0 + 2 * per, :], NN)
+        imag = jnp.where((lane & per) == 0, imag, -imag)
+        both = jnp.concatenate([real, imag], axis=0).astype(BF16)[:, :wide]
+        acc = acc + dot(both, select_ref[p * wide : (p + 1) * wide, :], NN)
     for p in range(2):
         i0 = (6 + p) * per
-        z = z_ref[6 + p]
-        real = dot(z, cos_ref[i0 : i0 + per, :], NT)
-        imag = -dot(z, sin_ref[i0 : i0 + per, :], NT)
-        both = jnp.concatenate([real, imag], axis=0).astype(BF16)
-        acc = acc + dot(both, select[i0 : i0 + per, :], NN)
+        d = dot(z_ref[6 + p], trig_ref[2 * i0 : 2 * (i0 + per), :], NT)
+        both = jnp.concatenate([d[:, :per], -d[:, per:]], axis=0).astype(BF16)
+        acc = acc + dot(both, select_ref[i0 : i0 + per, :], NN)
     out_ref[...] = acc.T.astype(BF16)
-    loads[3].wait()
+    loads[5].wait()
 
 
 def fold_kernel(in_ref, out_ref, x_ref):
@@ -152,40 +173,46 @@
                     out_ref[copy, row : row + 16, :] = tile
 
 
-def legendre_kernel(x_ref, table_ref, damping_ref, assign_ref, limit_ref, spectra_ref, out_ref, wide_ref, sums_ref, *, top):
+def legendre_kernel(x_ref, table_ref, scale_ref, spectra_ref, out_ref, wide_ref, sums_ref):
     pairs, degrees, half_lat = table_ref.shape
     columns = spectra_ref.shape[1]
     slots = pairs // 2
     groups = half_lat // 128
     stride = pairs * groups
-    slot0 = lax.axis_index("lat") * slots
-    first = lax.axis_index("fld") * degrees
-    wide_ref[...] = x_ref[...].astype(F32)
-    field = lax.broadcasted_iota(jnp.int32, (columns, degrees), 0) // 2
-    damp = jnp.zeros((columns, degrees), F32)
-    for n in range(columns // 2):
-        damp = jnp.where(field == n, damping_ref[n], damp)
-    pair_index = first + lax.broadcasted_iota(jnp.int32, (columns, degrees), 1)
+
+    def widen(s):
+        for n in range(columns):
+            at = slice(n * stride + 2 * s * groups, n * stride + 2 * (s + 1) * groups)
+            wide_ref[at, :] = x_ref[at, :].astype(F32)
+
+    def narrow(s):
+        for n in range(columns):
+            at = slice(n * stride + 2 * s * groups, n * stride + 2 * (s + 1) * groups)
+            out_ref[at, :] = sums_ref[at, :].astype(BF16)
+
+    def analyse(sa):
+        rows = [wide_ref[pl.ds(sa * groups + g, columns, stride=stride), :] for g in range(groups)]
+        return dot(jnp.concatenate(rows, axis=1).astype(BF16), table_ref[sa], NT)
+
+    def synthesise(sa, coefficient):
+        diffused = (coefficient * scale_ref[sa]).astype(BF16)
+        spectra_ref[sa] = diffused
+        back = dot(diffused, table_ref[sa], NN)
+        for g in range(groups):
+            sums_ref[pl.ds(sa * groups + g, columns, stride=stride), :] = back[:, g * 128 : g * 128 + 128]
+
+    widen(0)
+    coefficients = [analyse(0), analyse(1)]
     for s in range(slots):
-        wave = assign_ref[slot0 + s]
-        limit = limit_ref[wave]
+        if s + 1 < slots:
+            widen(s + 1)
         for a in range(2):
-            sa = 2 * s + a
-            rows = jnp.concatenate(
-                [wide_ref[pl.ds(sa * groups + g, columns, stride=stride), :] for g in range(groups)], axis=1
-            ).astype(BF16)
-            table = table_ref[sa]
-            coefficient = dot(rows, table, NT)
-            offset = 2 * pair_index + a
-            degree = (wave + 1 + offset).astype(F32)
-            ratio = degree * (degree + 1.0) / float(top * (top + 1))
-            scaled = coefficient / (1.0 + damp * (ratio * ratio))
-            diffused = jnp.where(offset < limit, scaled, 0.0).astype(BF16)
-            spectra_ref[sa] = diffused
-            back = dot(diffused, table, NN)
-            for g in range(groups):
-                sums_ref[pl.ds(sa * groups + g, columns, stride=stride), :] = back[:, g * 128 : g * 128 + 128]
-    out_ref[...] = sums_ref[...].astype(BF16)
+            if s + 1 < slots:
+                coefficients.append(analyse(2 * s + 2 + a))
+            synthesise(2 * s + a, coefficients[2 * s + a])
+        if s > 0:
+            narrow(s - 1)
+    narrow(slots - 1)
 
 
 def unfold_kernel(in_ref, out_ref, y_ref):
@@ -219,30 +246,33 @@
     out_ref[...] = y_ref[...].astype(BF16)
 
 
-def inverse_kernel(in_ref, assign_ref, cos_ref, sin_ref, out_hbm, w_ref, out_ref, sems):
+def inverse_kernel(in_ref, select_ref, trig_ref, out_hbm, w_ref, out_ref, sems):
     rows, lon_count = out_ref.shape
-    waves, span = cos_ref.shape
+    waves = select_ref.shape[0]
+    span = trig_ref.shape[1]
     per = waves // RADIX
-    select = wave_select(assign_ref[...], waves)
     slots = in_ref[...].astype(F32).T.astype(BF16)
 
     def ordered(i0, count):
-        return dot(slots, select[i0 : i0 + count, :], NT)
+        part = select_ref[i0 : i0 + count, :]
+        both = dot(slots, jnp.concatenate([part, part], axis=0), NT)
+        lane = lax.broadcasted_iota(jnp.int32, (rows, 2 * count), 1)
+        return both[:rows], both[rows:], lane
 
     for p in range(3):
-        i0 = 2 * p * per
-        g = ordered(i0, 2 * per)
-        lane = lax.broadcasted_iota(jnp.int32, g.shape, 1)
-        line = lax.broadcasted_iota(jnp.int32, g.shape, 0)
-        g = jnp.where((lane >= per) & (line >= rows), -g, g).astype(BF16)
-        cc = dot(g, cos_ref[i0 : i0 + 2 * per, :], NN)
-        ss = dot(g, sin_ref[i0 : i0 + 2 * per, :], NN)
-        w_ref[2 * p] = cc[:rows] - ss[rows:]
-        w_ref[2 * p + 1] = ss[:rows] + cc[rows:]
+        wide = 2 * per
+        real, imag, lane = ordered(p * wide, wide)
+        imag = jnp.where((lane & per) == 0, imag, -imag)
+        first = lane < wide
+        g = jnp.concatenate([jnp.where(first, real, -imag), jnp.where(first, imag, real)], axis=0).astype(BF16)
+        w = dot(g, trig_ref[2 * p * wide : 2 * (p + 1) * wide, :], NN)
+        w_ref[2 * p] = w[:rows]
+        w_ref[2 * p + 1] = w[rows:]
     for p in range(2):
         i0 = (6 + p) * per
-        g = ordered(i0, per).astype(BF16)
-        w_ref[6 + p] = dot(g[:rows], cos_ref[i0 : i0 + per, :], NN) - dot(g[rows:], sin_ref[i0 : i0 + per, :], NN)
+        real, imag, lane = ordered(i0, per)
+        g = jnp.where(lane < per, real, -imag).astype(BF16)
+        w_ref[6 + p] = dot(g, trig_ref[2 * i0 : 2 * (i0 + per), :], NN)
 
     tile = 16
     width = 256
@@ -277,7 +307,6 @@
 
 
 VMEM = pl.BlockSpec(memory_space=pltpu.VMEM)
-SMEM = pl.BlockSpec(memory_space=pltpu.SMEM)
 HBM = pl.BlockSpec(memory_space=pltpu.HBM)
 
 
@@ -321,26 +350,33 @@
     wide = pltpu.VMEM((total_waves, 2 * rows), F32)
     gathered_wide = pltpu.VMEM((fld_devices * block, 128), F32)
 
-    sent, assign_row, cos_table, sin_table, table = call(
-        forward_kernel, "forward",
+    scalars = lambda array: in_hbm(array.reshape(1, array.shape[0]))
+    sent, select, trig, table, scale = call(
+        lambda *refs: forward_kernel(*refs, top=top), "forward",
         (
             by_wave,
-            pltpu.VMEM((1, total_waves), jnp.int32),
-            pltpu.VMEM((total_waves, span), BF16),
-            pltpu.VMEM((total_waves, span), BF16),
+            pltpu.VMEM((total_waves, total_waves), BF16),
+            pltpu.VMEM((2 * total_waves, span), BF16),
             pltpu.VMEM((pairs, pair_slots, half_lat), BF16),
+            pltpu.VMEM((pairs, columns, pair_slots), F32),
         ),
-        [HBM] * 5,
+        [HBM] * 6,
         [
             pltpu.VMEM((rows, lon_count), BF16),
             pltpu.VMEM((RADIX, rows, span), BF16),
-            pltpu.SemaphoreType.DMA((steps + 4,)),
+            pltpu.VMEM((1, total_waves), jnp.int32),
+            pltpu.SMEM((1, field_total), F32),
+            pltpu.SMEM((1, total_waves), jnp.int32),
+            pltpu.SMEM((1, total_waves), jnp.int32),
+            pltpu.SemaphoreType.DMA((steps + 6,)),
         ],
     )(
         in_hbm(fields.reshape(rows, lon_count)),
-        in_hbm(assignment.reshape(1, total_waves)),
-        *map(in_hbm, wave_tables(total_waves, lon_count)),
+        scalars(assignment),
+        in_hbm(wave_table(total_waves, lon_count)),
         in_hbm(legendre.reshape(pairs, pair_slots, half_lat)),
+        scalars(damping),
+        scalars(truncation),
     )
     received = lax.all_to_all(sent.reshape(lat_devices, wave_slots, 2 * rows), "lat", 0, 0, tiled=True)
     (copies,) = call(
@@ -348,26 +384,26 @@
     )(in_vmem(received.reshape(total_waves, 2 * rows)))
     gathered = lax.all_to_all(copies, "fld", 0, 0, tiled=True)
     spectra, partial = call(
-        lambda *refs: legendre_kernel(*refs, top=top), "legendre",
+        legendre_kernel, "legendre",
         (
             jax.ShapeDtypeStruct((pairs, columns, pair_slots), BF16),
             pltpu.VMEM((fld_devices * block, 128), BF16),
         ),
-        [VMEM, VMEM, SMEM, SMEM, SMEM],
+        [VMEM] * 3,
         [gathered_wide, gathered_wide],
-    )(in_vmem(gathered.reshape(fld_devices * block, 128)), in_vmem(table), damping, assignment, truncation)
+    )(in_vmem(gathered.reshape(fld_devices * block, 128)), in_vmem(table), in_vmem(scale))
     parts = lax.all_to_all(partial.reshape(fld_devices, block, 128), "fld", 0, 0, tiled=True)
     (outgoing,) = call(unfold_kernel, "unfold", (by_wave,), [VMEM], [wide])(in_vmem(parts))
     returned = lax.all_to_all(outgoing.reshape(lat_devices, wave_slots, 2 * rows), "lat", 0, 0, tiled=True)
     (field_out,) = call(
-        inverse_kernel, "inverse", (jax.ShapeDtypeStruct((rows, lon_count), BF16),), [VMEM] * 4,
+        inverse_kernel, "inverse", (jax.ShapeDtypeStruct((rows, lon_count), BF16),), [VMEM] * 3,
         [
             pltpu.VMEM((RADIX, rows, span), F32),
             pltpu.VMEM((rows, lon_count), BF16),
             pltpu.SemaphoreType.DMA((steps,)),
         ],
         (HBM,),
-    )(in_vmem(returned.reshape(total_waves, 2 * rows)), in_vmem(assign_row), in_vmem(cos_table), in_vmem(sin_table))
+    )(in_vmem(returned.reshape(total_waves, 2 * rows)), in_vmem(select), in_vmem(trig))
     return (
         field_out.reshape(field_count, lat_rows, lon_count),
         spectra.reshape(wave_slots, 2, field_total, 2, pair_slots),

time: 92.4 us -> 90 us (0.974)
  Pallas kernels: 9.79 us -> 7.41 us
    pallas_call x2, Pallas kernels: 7.08 us -> 4.8 us  [the longest x1 2.66 us: on_device(): call(lambda *refs: forward_kernel(*refs, top=top), 'forward', (by_wave, p...]
where the time goes in v3:
time: 90 us; the launch traced here: 89.7 us
  blocking collectives  81.6 us (91%)
  Pallas kernels  7.41 us (8%)
    all_to_all x1, blocking collectives, on_device(): lax.all_to_all(sent.reshape(lat_devices, wave_slots, 2 * rows), 'lat', 0,...  24.4 us
    all_to_all x1, blocking collectives, on_device(): gathered = lax.all_to_all(copies, 'fld', 0, 0, tiled=True)  23.3 us
    all_to_all x1, blocking collectives, on_device(): lax.all_to_all(partial.reshape(fld_devices, block, 128), 'fld', 0, 0, til...  17.3 us
    all_to_all x1, blocking collectives, on_device(): lax.all_to_all(outgoing.reshape(lat_devices, wave_slots, 2 * rows), 'lat'...  16.7 us
    pallas_call x1, Pallas kernels, on_device(): call(lambda *refs: forward_kernel(*refs, top=top), 'forward', (by_wave, p...  2.66 us
    pallas_call x1, Pallas kernels, on_device(): call(inverse_kernel, 'inverse', (jax.ShapeDtypeStruct((rows, lon_count),...  2.26 us
    pallas_call x1, Pallas kernels, on_device(): call(legendre_kernel, 'legendre', (jax.ShapeDtypeStruct((pairs, columns,...  2.14 us

profile of v3, /device:TPU:1, one launch (start us, length us, event | category | flops | bytes accessed | tf_op | source)
XLA Modules:
  0.0 89.7 jit_solution(1298120967313091250)
XLA Ops:
  0.6 2.7 %forward.1 = (bf16[256,128]{1,0:T(8,128)(2,1)S(1)}, bf16[256,256]{1,0:T(8,128)(2,1)S(1)}, bf16[512,1024]{1,0:T(8,128)(2,1)S(1)}, bf16[8,128,1024]{2,1,0:T(8,128)(2,1)S(1)}, f32[8,32,128]{2,1,0:T(8,128)S(1)}) custom-call(bf16[64,8192]{1,0:T(8,128)(2,1)} %bitcast.21, s32[1,256]{1,0:T(1,128)} %bitcast.22, bf16[512,1024]{1,0:T(8,128)(2,1)} %constant.2.clone.refs_2_, ...), custom_call_target="tpu_custom_call" | custom-call | tf_op jit(solution)/shard_map/forward/pallas_call | solution.py:354
  3.3 24.4 %all_to_all.20 = bf16[64,4,128]{2,1,0:T(4,128)(2,1)S(1)} all-to-all(bf16[64,4,128]{2,1,0:T(4,128)(2,1)S(1)} %bitcast.18), channel_id=1, replica_groups=mesh['lat'=64,'fld'=8] {'lat'}, dimensions={0} | all-to-all | bytes 131072 | tf_op jit(solution)/shard_map/all_to_all | solution.py:381
  27.7 0.2 fold.1
  27.8 23.3 %all_to_all.21 = bf16[8,256,128]{2,1,0:T(8,128)(2,1)S(1)} all-to-all(bf16[8,256,128]{2,1,0:T(8,128)(2,1)S(1)} %fold.1), channel_id=1, replica_groups=mesh['lat'=64,'fld'=8] {'fld'}, dimensions={0} | all-to-all | bytes 1048576 | tf_op jit(solution)/shard_map/all_to_all | solution.py:385
  51.1 2.1 %legendre.1 = (bf16[8,32,128]{2,1,0:T(8,128)(2,1)}, bf16[2048,128]{1,0:T(8,128)(2,1)S(1)}) custom-call(bf16[2048,128]{1,0:T(8,128)(2,1)S(1)} %bitcast.13, bf16[8,128,1024]{2,1,0:T(8,128)(2,1)S(1)} %get-tuple-element.10.table_ref, f32[8,32,128]{2,1,0:T(8,128)S(1)} %get-tuple-element.11.scale_ref), custom_call_target="tpu_custom_call" | custom-call | tf_op jit(solution)/shard_map/legendre/pallas_call | solution.py:386
  53.3 17.3 %all_to_all.22.in_ref = bf16[8,256,128]{2,1,0:T(8,128)(2,1)S(1)} all-to-all(bf16[8,256,128]{2,1,0:T(8,128)(2,1)S(1)} %bitcast.14), channel_id=1, replica_groups=mesh['lat'=64,'fld'=8] {'fld'}, dimensions={0} | all-to-all | bytes 1048576 | tf_op jit(solution)/shard_map/all_to_all | solution.py:395
  70.6 0.2 unfold.1
  70.8 16.7 %all_to_all.23 = bf16[64,4,128]{2,1,0:T(4,128)(2,1)S(1)} all-to-all(bf16[64,4,128]{2,1,0:T(4,128)(2,1)S(1)} %bitcast.17), channel_id=1, replica_groups=mesh['lat'=64,'fld'=8] {'lat'}, dimensions={0} | all-to-all | bytes 131072 | tf_op jit(solution)/shard_map/all_to_all | solution.py:397
  87.4 2.3 %inverse.1 = bf16[64,8192]{1,0:T(8,128)(2,1)} custom-call(bf16[256,128]{1,0:T(8,128)(2,1)S(1)} %bitcast.15, bf16[256,256]{1,0:T(8,128)(2,1)S(1)} %get-tuple-element.13.select_ref, bf16[512,1024]{1,0:T(8,128)(2,1)S(1)} %get-tuple-element.14.trig_ref), custom_call_target="tpu_custom_call" | custom-call | tf_op jit(solution)/shard_map/inverse/pallas_call | solution.py:398

commit v4 on v3

--- a/solution.py
+++ b/solution.py
@@ -136,59 +136,75 @@
         d = dot(z_ref[6 + p], trig_ref[2 * i0 : 2 * (i0 + per), :], NT)
         both = jnp.concatenate([d[:, :per], -d[:, per:]], axis=0).astype(BF16)
         acc = acc + dot(both, select_ref[i0 : i0 + per, :], NN)
-    out_ref[...] = acc.T.astype(BF16)
+    by_slot = acc.T
+    upper = lax.broadcasted_iota(jnp.int32, (8, 2 * rows), 0) < 4
+    repeats = out_ref.shape[0] // (4 * waves)
+    for n in range(waves // 8):
+        group = by_slot[8 * n : 8 * n + 8]
+        turned = pltpu.roll(group, 4, 0)
+        for m, both in enumerate((jnp.where(upper, group, turned), jnp.where(upper, turned, group))):
+            both = jnp.concatenate([both, both], axis=0).astype(BF16)
+            for k in range(repeats):
+                row = ((2 * n + m) * repeats + k) * 16
+                out_ref[row : row + 16, :] = both
     loads[5].wait()
 
 
-def fold_kernel(in_ref, out_ref, x_ref):
-    copies = out_ref.shape[0]
-    total = in_ref.shape[0]
-    slots = 4
-    half = total // 2
-    x_ref[...] = in_ref[...].astype(F32)
-    block = lax.broadcasted_iota(jnp.int32, (8, 128), 1) // 32
-    for s in range(slots):
-        folded = ([], [])
-        for part in range(4):
-            north = x_ref[pl.ds(4 * part + s, 8, stride=16), :]
-            south = x_ref[pl.ds(half + 4 * part + s, 8, stride=16), :]
-            folded[0].append((north + south) * 0.5)
-            folded[1].append((north - south) * 0.5)
-        for f in range(2):
-            for r in range(2):
-                source = 2 * r + f
-                pair = []
-                for a in range(2):
-                    rows = None
-                    for part in range(4):
-                        shift = (32 * (part - source)) % 128
-                        moved = folded[a][part]
-                        if shift:
-                            moved = pltpu.roll(moved, shift, 1)
-                        rows = moved if rows is None else jnp.where(block == part, moved, rows)
-                    pair.append(rows)
-                tile = jnp.concatenate(pair, axis=0).astype(BF16)
-                row = ((2 * f + r) * 8 + 2 * s) * 8
-                for copy in range(copies):
-                    out_ref[copy, row : row + 16, :] = tile
-
-
-def legendre_kernel(x_ref, table_ref, scale_ref, spectra_ref, out_ref, wide_ref, sums_ref):
+def block_transpose(rows):
+    block = lax.broadcasted_iota(jnp.int32, rows[0].shape, 1) // 32
+    low = block < 2
+    even = block % 2 == 0
+    half = [None] * 4
+    for n in range(2):
+        half[n] = jnp.where(low, rows[n], pltpu.roll(rows[n + 2], 64, 1))
+        half[n + 2] = jnp.where(low, pltpu.roll(rows[n], 64, 1), rows[n + 2])
+    out = [None] * 4
+    for n in (0, 2):
+        out[n] = jnp.where(even, half[n], pltpu.roll(half[n + 1], 32, 1))
+        out[n + 1] = jnp.where(even, pltpu.roll(half[n], 96, 1), half[n + 1])
+    return out
+
+
+def legendre_kernel(x_ref, table_ref, scale_ref, spectra_ref, out_ref, raw_ref, wide_ref, sums_ref, back_ref):
     pairs, degrees, half_lat = table_ref.shape
     columns = spectra_ref.shape[1]
     slots = pairs // 2
     groups = half_lat // 128
     stride = pairs * groups
-
-    def widen(s):
-        for n in range(columns):
-            at = slice(n * stride + 2 * s * groups, n * stride + 2 * (s + 1) * groups)
-            wide_ref[at, :] = x_ref[at, :].astype(F32)
-
-    def narrow(s):
-        for n in range(columns):
-            at = slice(n * stride + 2 * s * groups, n * stride + 2 * (s + 1) * groups)
-            out_ref[at, :] = sums_ref[at, :].astype(BF16)
+    owners = columns // 4
+    total = x_ref.shape[0]
+    half = total // 2
+    step = total // 2 // groups
+    piece = step // 4
+    order = ((0, 0), (0, 1), (1, 0), (1, 1))
+
+    def place(owner, r, f, sa):
+        return slice(((4 * owner + 2 * f + r) * pairs + sa) * groups, ((4 * owner + 2 * f + r) * pairs + sa + 1) * groups)
+
+    def fold(s):
+        for owner in range(owners):
+            folded = ([], [])
+            for part in range(4):
+                row = part * piece + slots * owner + s
+                north = raw_ref[pl.ds(row, groups, stride=step), :]
+                south = raw_ref[pl.ds(half + row, groups, stride=step), :]
+                folded[0].append((north + south) * 0.5)
+                folded[1].append((north - south) * 0.5)
+            for a in range(2):
+                for (r, f), rows in zip(order, block_transpose(folded[a])):
+                    wide_ref[place(owner, r, f, 2 * s + a), :] = rows
+
+    def unfold(s):
+        for owner in range(owners):
+            north, south = [], []
+            for r, f in order:
+                even = sums_ref[place(owner, r, f, 2 * s), :]
+                odd = sums_ref[place(owner, r, f, 2 * s + 1), :]
+                north.append(even + odd)
+                south.append(even - odd)
+            for base, rows in ((0, north), (half, south)):
+                for part, moved in enumerate(block_transpose(rows)):
+                    back_ref[pl.ds(base + part * piece + slots * owner + s, groups, stride=step), :] = moved
 
     def analyse(sa):
         rows = [wide_ref[pl.ds(sa * groups + g, columns, stride=stride), :] for g in range(groups)]
@@ -201,49 +217,20 @@
         for g in range(groups):
             sums_ref[pl.ds(sa * groups + g, columns, stride=stride), :] = back[:, g * 128 : g * 128 + 128]
 
-    widen(0)
+    raw_ref[...] = x_ref[...].astype(F32)
+    fold(0)
     coefficients = [analyse(0), analyse(1)]
     for s in range(slots):
         if s + 1 < slots:
-            widen(s + 1)
+            fold(s + 1)
         for a in range(2):
             if s + 1 < slots:
                 coefficients.append(analyse(2 * s + 2 + a))
             synthesise(2 * s + a, coefficients[2 * s + a])
         if s > 0:
-            narrow(s - 1)
-    narrow(slots - 1)
-
-
-def unfold_kernel(in_ref, out_ref, y_ref):
-    sources, total, _ = in_ref.shape
-    half = total // 2
-    block = lax.broadcasted_iota(jnp.int32, (8, 128), 1) // 32
-
-    def summed(row):
-        acc = in_ref[0, row : row + 16, :].astype(F32)
-        for n in range(1, sources):
-            acc = acc + in_ref[n, row : row + 16, :].astype(F32)
-        return acc.astype(BF16).astype(F32)
-
-    for s in range(4):
-        north, south = {}, {}
-        for f in range(2):
-            for r in range(2):
-                both = summed(((2 * f + r) * 8 + 2 * s) * 8)
-                north[2 * r + f] = both[:8] + both[8:]
-                south[2 * r + f] = both[:8] - both[8:]
-        for part in range(4):
-            for base, rows_of in ((0, north), (half, south)):
-                rows = None
-                for target in range(4):
-                    shift = (32 * (target - part)) % 128
-                    moved = rows_of[target]
-                    if shift:
-                        moved = pltpu.roll(moved, shift, 1)
-                    rows = moved if rows is None else jnp.where(block == target, moved, rows)
-                y_ref[pl.ds(base + 4 * part + s, 8, stride=16), :] = rows
-    out_ref[...] = y_ref[...].astype(BF16)
+            unfold(s - 1)
+    unfold(slots - 1)
+    out_ref[...] = back_ref[...].astype(BF16)
 
 
 def inverse_kernel(in_ref, select_ref, trig_ref, out_hbm, w_ref, out_ref, sems):
@@ -251,7 +238,19 @@
     waves = select_ref.shape[0]
     span = trig_ref.shape[1]
     per = waves // RADIX
-    slots = in_ref[...].astype(F32).T.astype(BF16)
+    upper = lax.broadcasted_iota(jnp.int32, (8, 2 * rows), 0) < 4
+    size = in_ref.shape[0] * 4 // waves
+
+    def summed(n):
+        acc = None
+        for row in range(n * size, (n + 1) * size, 16):
+            both = in_ref[row : row + 16, :].astype(F32)
+            both = both[:8] + both[8:]
+            acc = both if acc is None else acc + both
+        return acc + pltpu.roll(acc, 4, 0)
+
+    slots = [jnp.where(upper, summed(2 * n), summed(2 * n + 1)) for n in range(waves // 8)]
+    slots = jnp.concatenate(slots, axis=0).T.astype(BF16)
 
     def ordered(i0, count):
         part = select_ref[i0 : i0 + count, :]
@@ -345,16 +344,19 @@
     top = total_waves + 2 * pair_slots * fld_devices - 1
     span = lon_count // RADIX
     steps = rows // 16
-    block = total_waves * 2 * rows // 128
-    by_wave = pltpu.VMEM((total_waves, 2 * rows), BF16)
-    wide = pltpu.VMEM((total_waves, 2 * rows), F32)
-    gathered_wide = pltpu.VMEM((fld_devices * block, 128), F32)
+    total = fld_devices * total_waves
+    message = pltpu.VMEM((total, 2 * rows), BF16)
+
+    def exchange(array):
+        array = array.reshape(lat_devices * fld_devices, wave_slots, 2 * rows)
+        return in_vmem(lax.all_to_all(array, ("lat", "fld"), 0, 0, tiled=True).reshape(total, 2 * rows))
+
 
     scalars = lambda array: in_hbm(array.reshape(1, array.shape[0]))
     sent, select, trig, table, scale = call(
         lambda *refs: forward_kernel(*refs, top=top), "forward",
         (
-            by_wave,
+            message,
             pltpu.VMEM((total_waves, total_waves), BF16),
             pltpu.VMEM((2 * total_waves, span), BF16),
             pltpu.VMEM((pairs, pair_slots, half_lat), BF16),
@@ -378,23 +380,10 @@
         scalars(damping),
         scalars(truncation),
     )
-    received = lax.all_to_all(sent.reshape(lat_devices, wave_slots, 2 * rows), "lat", 0, 0, tiled=True)
-    (copies,) = call(
-        fold_kernel, "fold", (pltpu.VMEM((fld_devices, block, 128), BF16),), [VMEM], [wide]
-    )(in_vmem(received.reshape(total_waves, 2 * rows)))
-    gathered = lax.all_to_all(copies, "fld", 0, 0, tiled=True)
     spectra, partial = call(
-        legendre_kernel, "legendre",
-        (
-            jax.ShapeDtypeStruct((pairs, columns, pair_slots), BF16),
-            pltpu.VMEM((fld_devices * block, 128), BF16),
-        ),
-        [VMEM] * 3,
-        [gathered_wide, gathered_wide],
-    )(in_vmem(gathered.reshape(fld_devices * block, 128)), in_vmem(table), in_vmem(scale))
-    parts = lax.all_to_all(partial.reshape(fld_devices, block, 128), "fld", 0, 0, tiled=True)
-    (outgoing,) = call(unfold_kernel, "unfold", (by_wave,), [VMEM], [wide])(in_vmem(parts))
-    returned = lax.all_to_all(outgoing.reshape(lat_devices, wave_slots, 2 * rows), "lat", 0, 0, tiled=True)
+        legendre_kernel, "legendre", (jax.ShapeDtypeStruct((pairs, columns, pair_slots), BF16), message),
+        [VMEM] * 3, [pltpu.VMEM((total, 2 * rows), F32)] * 4,
+    )(exchange(sent), in_vmem(table), in_vmem(scale))
     (field_out,) = call(
         inverse_kernel, "inverse", (jax.ShapeDtypeStruct((rows, lon_count), BF16),), [VMEM] * 3,
         [
@@ -403,7 +392,7 @@
             pltpu.SemaphoreType.DMA((steps,)),
         ],
         (HBM,),
-    )(in_vmem(returned.reshape(total_waves, 2 * rows)), in_vmem(select), in_vmem(trig))
+    )(exchange(partial), in_vmem(select), in_vmem(trig))
     return (
         field_out.reshape(field_count, lat_rows, lon_count),
         spectra.reshape(wave_slots, 2, field_total, 2, pair_slots),

time: 90 us -> 85.3 us (0.948)
  blocking collectives: 81.6 us -> 75.2 us
  Pallas kernels: 7.41 us -> 9.3 us
    all_to_all x4 -> x2, blocking collectives: 81.6 us -> 75.2 us  [exchange(): lax.all_to_all(array, ('lat', 'fld'), 0, 0, tiled=True)]
    pallas_call x1, Pallas kernels: 2.14 us -> 4.32 us  [on_device(): call(legendre_kernel, 'legendre', (jax.ShapeDtypeStruct((pairs, columns,...]
    pallas_call x3 -> x1, Pallas kernels: 3.02 us -> 2.67 us  [on_device(): call(lambda *refs: forward_kernel(*refs, top=top), 'forward', (message, p...]
where the time goes in v4:
time: 85.3 us; the launch traced here: 85.1 us
  blocking collectives  75.2 us (88%)
  Pallas kernels  9.3 us (11%)
    all_to_all x2, blocking collectives, exchange(): lax.all_to_all(array, ('lat', 'fld'), 0, 0, tiled=True)  75.2 us
    pallas_call x1, Pallas kernels, on_device(): call(legendre_kernel, 'legendre', (jax.ShapeDtypeStruct((pairs, columns,...  4.32 us
    pallas_call x1, Pallas kernels, on_device(): call(lambda *refs: forward_kernel(*refs, top=top), 'forward', (message, p...  2.67 us
    pallas_call x1, Pallas kernels, on_device(): call(inverse_kernel, 'inverse', (jax.ShapeDtypeStruct((rows, lon_count),...  2.31 us

profile of v4, /device:TPU:1, one launch (start us, length us, event | category | flops | bytes accessed | tf_op | source)
XLA Modules:
  0.0 85.1 jit_solution(2465854932048956186)
XLA Ops:
  0.6 2.7 %forward.1 = (bf16[2048,128]{1,0:T(8,128)(2,1)S(1)}, bf16[256,256]{1,0:T(8,128)(2,1)S(1)}, bf16[512,1024]{1,0:T(8,128)(2,1)S(1)}, bf16[8,128,1024]{2,1,0:T(8,128)(2,1)S(1)}, f32[8,32,128]{2,1,0:T(8,128)S(1)}) custom-call(bf16[64,8192]{1,0:T(8,128)(2,1)} %bitcast.17, s32[1,256]{1,0:T(1,128)} %bitcast.18, bf16[512,1024]{1,0:T(8,128)(2,1)} %constant.2.clone.refs_2_, ...), custom_call_target="tpu_custom_call" | custom-call | tf_op jit(solution)/shard_map/forward/pallas_call | solution.py:356
  3.3 43.8 %all_to_all.10 = bf16[512,4,128]{2,1,0:T(4,128)(2,1)S(1)} all-to-all(bf16[512,4,128]{2,1,0:T(4,128)(2,1)S(1)} %bitcast.13), channel_id=1, replica_groups=mesh['lat'=64,'fld'=8] {'lat','fld'}, dimensions={0} | all-to-all | bytes 1048576 | tf_op jit(solution)/shard_map/all_to_all | solution.py:352
  47.1 4.3 %legendre.1 = (bf16[8,32,128]{2,1,0:T(8,128)(2,1)}, bf16[2048,128]{1,0:T(8,128)(2,1)S(1)}) custom-call(bf16[2048,128]{1,0:T(8,128)(2,1)S(1)} %bitcast.11, bf16[8,128,1024]{2,1,0:T(8,128)(2,1)S(1)} %get-tuple-element.10.table_ref, f32[8,32,128]{2,1,0:T(8,128)S(1)} %get-tuple-element.11.scale_ref), custom_call_target="tpu_custom_call" | custom-call | tf_op jit(solution)/shard_map/legendre/pallas_call | solution.py:383
  51.4 31.4 %all_to_all.11 = bf16[512,4,128]{2,1,0:T(4,128)(2,1)S(1)} all-to-all(bf16[512,4,128]{2,1,0:T(4,128)(2,1)S(1)} %bitcast.14), channel_id=1, replica_groups=mesh['lat'=64,'fld'=8] {'lat','fld'}, dimensions={0} | all-to-all | bytes 1048576 | tf_op jit(solution)/shard_map/all_to_all | solution.py:352
  82.8 2.3 %inverse.1 = bf16[64,8192]{1,0:T(8,128)(2,1)} custom-call(bf16[2048,128]{1,0:T(8,128)(2,1)S(1)} %bitcast.12, bf16[256,256]{1,0:T(8,128)(2,1)S(1)} %get-tuple-element.13.select_ref, bf16[512,1024]{1,0:T(8,128)(2,1)S(1)} %get-tuple-element.14.trig_ref), custom_call_target="tpu_custom_call" | custom-call | tf_op jit(solution)/shard_map/inverse/pallas_call | solution.py:387

commit v5 on v4

--- a/solution.py
+++ b/solution.py
@@ -61,36 +61,6 @@
     for step in range(steps):
         rows_copy(step).start()
     loads[4].start()
-    for load in loads[:4]:
-        load.wait()
-
-    pairs, columns, degrees = scale_ref.shape
-    slots = pairs // 2
-    slot0 = lax.axis_index("lat") * slots
-    first = lax.axis_index("fld") * degrees
-    field = lax.broadcasted_iota(jnp.int32, (columns, degrees), 0) // 2
-    damp = jnp.zeros((columns, degrees), F32)
-    for n in range(columns // 2):
-        damp = jnp.where(field == n, damping_ref[0, n], damp)
-    pair_index = first + lax.broadcasted_iota(jnp.int32, (8, degrees), 1)
-    for s in range(slots):
-        wave = slot_ref[0, slot0 + s]
-        limit = limit_ref[0, wave]
-        for a in range(2):
-            offset = 2 * pair_index + a
-            degree = (wave + 1 + offset).astype(F32)
-            ratio = degree * (degree + 1.0) / float(top * (top + 1))
-            square = ratio * ratio
-            kept = offset < limit
-            for c in range(0, columns, 8):
-                factor = 1.0 / (1.0 + damp[c : c + 8] * square)
-                scale_ref[2 * s + a, c : c + 8, :] = jnp.where(kept, factor, 0.0)
-
-    wave_of = RADIX * lax.broadcasted_iota(jnp.int32, (per, waves), 0) - 1
-    for n, cls in enumerate(CLASS_ORDER):
-        hit = (wave_of + cls) == assign_ref[...]
-        select_ref[n * per : (n + 1) * per, :] = jnp.where(hit, 1.0, 0.0).astype(BF16)
-
     loads[5].start()
 
     def fold_rows(step, carry):
@@ -118,6 +88,36 @@
         return carry
 
     lax.fori_loop(0, steps, fold_rows, 0)
+    for load in loads[:4]:
+        load.wait()
+
+    pairs, columns, degrees = scale_ref.shape
+    slots = pairs // 2
+    slot0 = lax.axis_index("lat") * slots
+    first = lax.axis_index("fld") * degrees
+    field = lax.broadcasted_iota(jnp.int32, (columns, degrees), 0) // 2
+    damp = jnp.zeros((columns, degrees), F32)
+    for n in range(columns // 2):
+        damp = jnp.where(field == n, damping_ref[0, n], damp)
+    pair_index = first + lax.broadcasted_iota(jnp.int32, (8, degrees), 1)
+    for s in range(slots):
+        wave = slot_ref[0, slot0 + s]
+        limit = limit_ref[0, wave]
+        for a in range(2):
+            offset = 2 * pair_index + a
+            degree = (wave + 1 + offset).astype(F32)
+            ratio = degree * (degree + 1.0) / float(top * (top + 1))
+            square = ratio * ratio
+            kept = offset < limit
+            for c in range(0, columns, 8):
+                factor = 0.5 / (1.0 + damp[c : c + 8] * square)
+                scale_ref[2 * s + a, c : c + 8, :] = jnp.where(kept, factor, 0.0)
+
+    wave_of = RADIX * lax.broadcasted_iota(jnp.int32, (per, waves), 0) - 1
+    for n, cls in enumerate(CLASS_ORDER):
+        hit = (wave_of + cls) == assign_ref[...]
+        select_ref[n * per : (n + 1) * per, :] = jnp.where(hit, 1.0, 0.0).astype(BF16)
+
     loads[4].wait()
     acc = jnp.zeros((2 * rows, waves), F32)
     for p in range(3):
@@ -150,87 +150,74 @@
     loads[5].wait()
 
 
-def block_transpose(rows):
-    block = lax.broadcasted_iota(jnp.int32, rows[0].shape, 1) // 32
-    low = block < 2
-    even = block % 2 == 0
-    half = [None] * 4
-    for n in range(2):
-        half[n] = jnp.where(low, rows[n], pltpu.roll(rows[n + 2], 64, 1))
-        half[n + 2] = jnp.where(low, pltpu.roll(rows[n], 64, 1), rows[n + 2])
-    out = [None] * 4
-    for n in (0, 2):
-        out[n] = jnp.where(even, half[n], pltpu.roll(half[n + 1], 32, 1))
-        out[n + 1] = jnp.where(even, pltpu.roll(half[n], 96, 1), half[n + 1])
-    return out
-
-
-def legendre_kernel(x_ref, table_ref, scale_ref, spectra_ref, out_ref, raw_ref, wide_ref, sums_ref, back_ref):
+def swap_index(rows, axis, unit):
+    size = rows[0].shape[axis]
+    index = lax.broadcasted_iota(jnp.int32, rows[0].shape, axis) // unit
+    rows = list(rows)
+    for bit in (2, 1):
+        keep = (index & bit) == 0
+        for n in range(4):
+            if n & bit == 0:
+                low, high = rows[n], rows[n + bit]
+                rows[n] = jnp.where(keep, low, pltpu.roll(high, bit * unit, axis))
+                rows[n + bit] = jnp.where(keep, pltpu.roll(low, size - bit * unit, axis), high)
+    return rows
+
+
+def swap_middle(rows):
+    return [rows[0], rows[2], rows[1], rows[3]]
+
+
+def legendre_kernel(x_ref, table_ref, scale_ref, spectra_ref, out_ref, rows_ref, back_ref):
     pairs, degrees, half_lat = table_ref.shape
     columns = spectra_ref.shape[1]
     slots = pairs // 2
     groups = half_lat // 128
-    stride = pairs * groups
-    owners = columns // 4
-    total = x_ref.shape[0]
-    half = total // 2
-    step = total // 2 // groups
-    piece = step // 4
-    order = ((0, 0), (0, 1), (1, 0), (1, 1))
-
-    def place(owner, r, f, sa):
-        return slice(((4 * owner + 2 * f + r) * pairs + sa) * groups, ((4 * owner + 2 * f + r) * pairs + sa + 1) * groups)
-
-    def fold(s):
-        for owner in range(owners):
-            folded = ([], [])
+    half = x_ref.shape[0] // 2
+    tile = 16
+
+    def fold(at, g):
+        north, south = [], []
+        for part in range(4):
+            row = (4 * g + part) * columns + at
+            north.append(x_ref[row : row + tile, :].astype(F32))
+            south.append(x_ref[half + row : half + row + tile, :].astype(F32))
+        for a in range(2):
+            both = [n + t if a == 0 else n - t for n, t in zip(north, south)]
+            done = []
+            for h in (0, 8):
+                by_column = swap_middle(swap_index([v[h : h + 8] for v in both], 1, 32))
+                done.append(swap_index(by_column, 0, 1))
+            for s in range(slots):
+                rows_ref[2 * s + a, at : at + tile, 128 * g : 128 * g + 128] = jnp.concatenate(
+                    [done[0][s], done[1][s]], axis=0
+                ).astype(BF16)
+
+    def unfold(at, g):
+        view = (slice(at, at + tile), slice(128 * g, 128 * g + 128))
+        even = [back_ref[(2 * s, *view)] for s in range(slots)]
+        odd = [back_ref[(2 * s + 1, *view)] for s in range(slots)]
+        for base in (0, half):
+            both = [e + o if base == 0 else e - o for e, o in zip(even, odd)]
+            done = []
+            for h in (0, 8):
+                by_column = swap_middle(swap_index([v[h : h + 8] for v in both], 0, 1))
+                done.append(swap_index(by_column, 1, 32))
             for part in range(4):
-                row = part * piece + slots * owner + s
-                north = raw_ref[pl.ds(row, groups, stride=step), :]
-                south = raw_ref[pl.ds(half + row, groups, stride=step), :]
-                folded[0].append((north + south) * 0.5)
-                folded[1].append((north - south) * 0.5)
-            for a in range(2):
-                for (r, f), rows in zip(order, block_transpose(folded[a])):
-                    wide_ref[place(owner, r, f, 2 * s + a), :] = rows
-
-    def unfold(s):
-        for owner in range(owners):
-            north, south = [], []
-            for r, f in order:
-                even = sums_ref[place(owner, r, f, 2 * s), :]
-                odd = sums_ref[place(owner, r, f, 2 * s + 1), :]
-                north.append(even + odd)
-                south.append(even - odd)
-            for base, rows in ((0, north), (half, south)):
-                for part, moved in enumerate(block_transpose(rows)):
-                    back_ref[pl.ds(base + part * piece + slots * owner + s, groups, stride=step), :] = moved
-
-    def analyse(sa):
-        rows = [wide_ref[pl.ds(sa * groups + g, columns, stride=stride), :] for g in range(groups)]
-        return dot(jnp.concatenate(rows, axis=1).astype(BF16), table_ref[sa], NT)
-
-    def synthesise(sa, coefficient):
+                row = base + (4 * g + part) * columns + at
+                out_ref[row : row + tile, :] = jnp.concatenate([done[0][part], done[1][part]], axis=0).astype(BF16)
+
+    for g in range(groups):
+        for at in range(0, columns, tile):
+            fold(at, g)
+    for sa in range(pairs):
+        coefficient = dot(rows_ref[sa], table_ref[sa], NT)
         diffused = (coefficient * scale_ref[sa]).astype(BF16)
         spectra_ref[sa] = diffused
-        back = dot(diffused, table_ref[sa], NN)
-        for g in range(groups):
-            sums_ref[pl.ds(sa * groups + g, columns, stride=stride), :] = back[:, g * 128 : g * 128 + 128]
-
-    raw_ref[...] = x_ref[...].astype(F32)
-    fold(0)
-    coefficients = [analyse(0), analyse(1)]
-    for s in range(slots):
-        if s + 1 < slots:
-            fold(s + 1)
-        for a in range(2):
-            if s + 1 < slots:
-                coefficients.append(analyse(2 * s + 2 + a))
-            synthesise(2 * s + a, coefficients[2 * s + a])
-        if s > 0:
-            unfold(s - 1)
-    unfold(slots - 1)
-    out_ref[...] = back_ref[...].astype(BF16)
+        back_ref[sa] = dot(diffused, table_ref[sa], NN)
+    for g in range(groups):
+        for at in range(0, columns, tile):
+            unfold(at, g)
 
 
 def inverse_kernel(in_ref, select_ref, trig_ref, out_hbm, w_ref, out_ref, sems):
@@ -382,7 +369,7 @@
     )
     spectra, partial = call(
         legendre_kernel, "legendre", (jax.ShapeDtypeStruct((pairs, columns, pair_slots), BF16), message),
-        [VMEM] * 3, [pltpu.VMEM((total, 2 * rows), F32)] * 4,
+        [VMEM] * 3, [pltpu.VMEM((pairs, columns, half_lat), BF16), pltpu.VMEM((pairs, columns, half_lat), F32)],
     )(exchange(sent), in_vmem(table), in_vmem(scale))
     (field_out,) = call(
         inverse_kernel, "inverse", (jax.ShapeDtypeStruct((rows, lon_count), BF16),), [VMEM] * 3,

time: 85.3 us -> 84.3 us (0.988)
  Pallas kernels: 9.3 us -> 8.28 us
    pallas_call x1, Pallas kernels: 4.32 us -> 3.28 us  [on_device(): call(legendre_kernel, 'legendre', (jax.ShapeDtypeStruct((pairs, columns,...]
where the time goes in v5:
time: 84.3 us; the launch traced here: 84.1 us
  blocking collectives  75.2 us (89%)
  Pallas kernels  8.28 us (10%)
    all_to_all x2, blocking collectives, exchange(): lax.all_to_all(array, ('lat', 'fld'), 0, 0, tiled=True)  75.2 us
    pallas_call x1, Pallas kernels, on_device(): call(legendre_kernel, 'legendre', (jax.ShapeDtypeStruct((pairs, columns,...  3.28 us
    pallas_call x1, Pallas kernels, on_device(): call(lambda *refs: forward_kernel(*refs, top=top), 'forward', (message, p...  2.68 us
    pallas_call x1, Pallas kernels, on_device(): call(inverse_kernel, 'inverse', (jax.ShapeDtypeStruct((rows, lon_count),...  2.32 us

profile of v5, /device:TPU:1, one launch (start us, length us, event | category | flops | bytes accessed | tf_op | source)
XLA Modules:
  0.0 84.1 jit_solution(14527105747491726128)
XLA Ops:
  0.6 2.7 %forward.1 = (bf16[2048,128]{1,0:T(8,128)(2,1)S(1)}, bf16[256,256]{1,0:T(8,128)(2,1)S(1)}, bf16[512,1024]{1,0:T(8,128)(2,1)S(1)}, bf16[8,128,1024]{2,1,0:T(8,128)(2,1)S(1)}, f32[8,32,128]{2,1,0:T(8,128)S(1)}) custom-call(bf16[64,8192]{1,0:T(8,128)(2,1)} %bitcast.17, s32[1,256]{1,0:T(1,128)} %bitcast.18, bf16[512,1024]{1,0:T(8,128)(2,1)} %constant.2.clone.refs_2_, ...), custom_call_target="tpu_custom_call" | custom-call | tf_op jit(solution)/shard_map/forward/pallas_call | solution.py:343
  3.3 43.8 %all_to_all.10 = bf16[512,4,128]{2,1,0:T(4,128)(2,1)S(1)} all-to-all(bf16[512,4,128]{2,1,0:T(4,128)(2,1)S(1)} %bitcast.13), channel_id=1, replica_groups=mesh['lat'=64,'fld'=8] {'lat','fld'}, dimensions={0} | all-to-all | bytes 1048576 | tf_op jit(solution)/shard_map/all_to_all | solution.py:339
  47.1 3.3 %legendre.1 = (bf16[8,32,128]{2,1,0:T(8,128)(2,1)}, bf16[2048,128]{1,0:T(8,128)(2,1)S(1)}) custom-call(bf16[2048,128]{1,0:T(8,128)(2,1)S(1)} %bitcast.11, bf16[8,128,1024]{2,1,0:T(8,128)(2,1)S(1)} %get-tuple-element.10.table_ref, f32[8,32,128]{2,1,0:T(8,128)S(1)} %get-tuple-element.11.scale_ref), custom_call_target="tpu_custom_call" | custom-call | tf_op jit(solution)/shard_map/legendre/pallas_call | solution.py:370
  50.4 31.4 %all_to_all.11 = bf16[512,4,128]{2,1,0:T(4,128)(2,1)S(1)} all-to-all(bf16[512,4,128]{2,1,0:T(4,128)(2,1)S(1)} %bitcast.14), channel_id=1, replica_groups=mesh['lat'=64,'fld'=8] {'lat','fld'}, dimensions={0} | all-to-all | bytes 1048576 | tf_op jit(solution)/shard_map/all_to_all | solution.py:339
  81.8 2.3 %inverse.1 = bf16[64,8192]{1,0:T(8,128)(2,1)} custom-call(bf16[2048,128]{1,0:T(8,128)(2,1)S(1)} %bitcast.12, bf16[256,256]{1,0:T(8,128)(2,1)S(1)} %get-tuple-element.13.select_ref, bf16[512,1024]{1,0:T(8,128)(2,1)S(1)} %get-tuple-element.14.trig_ref), custom_call_target="tpu_custom_call" | custom-call | tf_op jit(solution)/shard_map/inverse/pallas_call | solution.py:374

commit v6 on v5

--- a/solution.py
+++ b/solution.py
@@ -194,25 +194,27 @@
                 ).astype(BF16)
 
     def unfold(at, g):
-        view = (slice(at, at + tile), slice(128 * g, 128 * g + 128))
-        even = [back_ref[(2 * s, *view)] for s in range(slots)]
-        odd = [back_ref[(2 * s + 1, *view)] for s in range(slots)]
-        for base in (0, half):
-            both = [e + o if base == 0 else e - o for e, o in zip(even, odd)]
-            done = []
-            for h in (0, 8):
-                by_column = swap_middle(swap_index([v[h : h + 8] for v in both], 0, 1))
-                done.append(swap_index(by_column, 1, 32))
+        lanes = slice(128 * g, 128 * g + 128)
+        done = ([], [])
+        for h in (0, 8):
+            lines = slice(at + h, at + h + 8)
+            even = [back_ref[2 * s, lines, lanes] for s in range(slots)]
+            odd = [back_ref[2 * s + 1, lines, lanes] for s in range(slots)]
+            for n in range(2):
+                both = [e + o if n == 0 else e - o for e, o in zip(even, odd)]
+                done[n].append(swap_index(swap_middle(swap_index(both, 0, 1)), 1, 32))
+        for n in range(2):
             for part in range(4):
-                row = base + (4 * g + part) * columns + at
-                out_ref[row : row + tile, :] = jnp.concatenate([done[0][part], done[1][part]], axis=0).astype(BF16)
+                row = n * half + (4 * g + part) * columns + at
+                pair = [moved[part] for moved in done[n]]
+                out_ref[row : row + tile, :] = jnp.concatenate(pair, axis=0).astype(BF16)
 
     for g in range(groups):
         for at in range(0, columns, tile):
             fold(at, g)
+    coefficients = [dot(rows_ref[sa], table_ref[sa], NT) for sa in range(pairs)]
     for sa in range(pairs):
-        coefficient = dot(rows_ref[sa], table_ref[sa], NT)
-        diffused = (coefficient * scale_ref[sa]).astype(BF16)
+        diffused = (coefficients[sa] * scale_ref[sa]).astype(BF16)
         spectra_ref[sa] = diffused
         back_ref[sa] = dot(diffused, table_ref[sa], NN)
     for g in range(groups):

time: 84.3 us -> 82.9 us (0.983)
  Pallas kernels: 8.28 us -> 6.79 us
    pallas_call x1, Pallas kernels: 3.28 us -> 1.8 us  [on_device(): call(legendre_kernel, 'legendre', (jax.ShapeDtypeStruct((pairs, columns,...]
where the time goes in v6:
time: 82.9 us; the launch traced here: 82.6 us
  blocking collectives  75.2 us (91%)
  Pallas kernels  6.79 us (8%)
    all_to_all x2, blocking collectives, exchange(): lax.all_to_all(array, ('lat', 'fld'), 0, 0, tiled=True)  75.2 us
    pallas_call x1, Pallas kernels, on_device(): call(lambda *refs: forward_kernel(*refs, top=top), 'forward', (message, p...  2.68 us
    pallas_call x1, Pallas kernels, on_device(): call(inverse_kernel, 'inverse', (jax.ShapeDtypeStruct((rows, lon_count),...  2.31 us
    pallas_call x1, Pallas kernels, on_device(): call(legendre_kernel, 'legendre', (jax.ShapeDtypeStruct((pairs, columns,...  1.8 us

profile of v6, /device:TPU:1, one launch (start us, length us, event | category | flops | bytes accessed | tf_op | source)
XLA Modules:
  0.0 82.6 jit_solution(11797025888225420952)
XLA Ops:
  0.6 2.7 %forward.1 = (bf16[2048,128]{1,0:T(8,128)(2,1)S(1)}, bf16[256,256]{1,0:T(8,128)(2,1)S(1)}, bf16[512,1024]{1,0:T(8,128)(2,1)S(1)}, bf16[8,128,1024]{2,1,0:T(8,128)(2,1)S(1)}, f32[8,32,128]{2,1,0:T(8,128)S(1)}) custom-call(bf16[64,8192]{1,0:T(8,128)(2,1)} %bitcast.17, s32[1,256]{1,0:T(1,128)} %bitcast.18, bf16[512,1024]{1,0:T(8,128)(2,1)} %constant.2.clone.refs_2_, ...), custom_call_target="tpu_custom_call" | custom-call | tf_op jit(solution)/shard_map/forward/pallas_call | solution.py:345
  3.3 43.8 %all_to_all.10 = bf16[512,4,128]{2,1,0:T(4,128)(2,1)S(1)} all-to-all(bf16[512,4,128]{2,1,0:T(4,128)(2,1)S(1)} %bitcast.13), channel_id=1, replica_groups=mesh['lat'=64,'fld'=8] {'lat','fld'}, dimensions={0} | all-to-all | bytes 1048576 | tf_op jit(solution)/shard_map/all_to_all | solution.py:341
  47.1 1.8 %legendre.1 = (bf16[8,32,128]{2,1,0:T(8,128)(2,1)}, bf16[2048,128]{1,0:T(8,128)(2,1)S(1)}) custom-call(bf16[2048,128]{1,0:T(8,128)(2,1)S(1)} %bitcast.11, bf16[8,128,1024]{2,1,0:T(8,128)(2,1)S(1)} %get-tuple-element.10.table_ref, f32[8,32,128]{2,1,0:T(8,128)S(1)} %get-tuple-element.11.scale_ref), custom_call_target="tpu_custom_call" | custom-call | tf_op jit(solution)/shard_map/legendre/pallas_call | solution.py:372
  48.9 31.4 %all_to_all.11 = bf16[512,4,128]{2,1,0:T(4,128)(2,1)S(1)} all-to-all(bf16[512,4,128]{2,1,0:T(4,128)(2,1)S(1)} %bitcast.14), channel_id=1, replica_groups=mesh['lat'=64,'fld'=8] {'lat','fld'}, dimensions={0} | all-to-all | bytes 1048576 | tf_op jit(solution)/shard_map/all_to_all | solution.py:341
  80.3 2.3 %inverse.1 = bf16[64,8192]{1,0:T(8,128)(2,1)} custom-call(bf16[2048,128]{1,0:T(8,128)(2,1)S(1)} %bitcast.12, bf16[256,256]{1,0:T(8,128)(2,1)S(1)} %get-tuple-element.13.select_ref, bf16[512,1024]{1,0:T(8,128)(2,1)S(1)} %get-tuple-element.14.trig_ref), custom_call_target="tpu_custom_call" | custom-call | tf_op jit(solution)/shard_map/inverse/pallas_call | solution.py:376
